TPU v7x, 512 devices: a whole 4x4x16 slice. The times are simulated.
512 devices in a mesh: win: 8 (over y, core), frame: 64 (over z, x).
Axes of the slice: x: 4, y: 4, z: 16, core: 2. Of those that a mesh axis runs over, the one named last changes fastest.
Arguments:
- distances: float32 [32, 131072], P(None, 'frame'), may hold values from 0.05 to 9
- sample_ids: int32 [131072], P('frame'), may hold values from 0 to 4095, as said below
- lengths: int32 [64], replicated, may hold values from 1 to 2048, 81920 in all
- stiffness: float32 [4096, 32], P('win'), may hold values from 0.5 to 19
- centers: float32 [4096, 32], P('win'), may hold values from 0.1 to 3.7
Outputs:
- free_energy: float32 [4096], P('win')
Inputs may be any that keep to these rules, and one draw needn't show every extreme that they name: The frames of a block occupy its first slots; the lengths add up to 81920 and the largest is 2048. `sample_ids`: slots beyond a block's length hold ids that are not used; exactly 512 windows appear in no slot.
All inputs are finite; a program needn't handle non-finite values.
Results may differ from a plain program's by a relative error of at most 0.0003.
Values sent between devices are 32-bit elements; how exact they have to be, the bound alone decides.
No kernel may reach another device: no remote copies, remote signals or barrier semaphores. Data moves between devices by JAX's collectives and lax.ppermute only.
A program may use at most 64 MiB of HBM per device.

v0:
```python
import jax
import jax.numpy as jnp
from jax import lax
from jax.sharding import PartitionSpec as P

ITERS = 2
BAL = 1280


floor_value = -1e30


def coefficients(stiffness, centers):
    constant = jnp.sum(0.5 * stiffness * centers * centers, axis=1, keepdims=True)
    return jnp.concatenate([constant, -stiffness * centers, 0.5 * stiffness], axis=1)


def features(separations):
    unit_row = jnp.ones((1, separations.shape[1]), separations.dtype)
    return jnp.concatenate([unit_row, separations, separations * separations], axis=0)


def energies(coef_rows, separations):
    return jnp.dot(
        coef_rows,
        features(separations),
        precision=lax.Precision.HIGHEST,
        preferred_element_type=jnp.float32,
    )


def pair_combine(earlier, latter):
    top_all = jnp.maximum(earlier[0], latter[0])
    merged = earlier[1] * jnp.exp(earlier[0] - top_all) + latter[1] * jnp.exp(latter[0] - top_all)
    return (top_all, merged)


def pick_block(slot_total):
    return 512 if slot_total % 512 == 0 else slot_total


def denominators(highest, summed):
    global_top = lax.pmax(highest, "win")
    summed = lax.psum(summed * jnp.exp(highest - global_top), "win")
    highest = global_top
    return highest + jnp.log(summed)


def window_totals(highest, summed):
    global_top = lax.pmax(highest, "frame")
    summed = lax.psum(summed * jnp.exp(highest - global_top), "frame")
    highest = global_top
    return -(highest + jnp.log(summed))


def on_device(distances, sample_ids, lengths, stiffness, centers):
    coef_rows = coefficients(stiffness, centers)
    local_windows = stiffness.shape[0]
    restraints, capacity = distances.shape
    my_index = lax.axis_index("frame")
    own_length = lax.dynamic_index_in_dim(lengths, my_index, keepdims=False)
    slot_index = jnp.arange(capacity, dtype=jnp.int32)
    slot_usable = slot_index < own_length
    numbers = lax.axis_index("win") * local_windows + jnp.arange(local_windows, dtype=jnp.int32)
    count_len = pick_block(capacity)
    id_blocks = sample_ids.reshape(capacity // count_len, count_len)
    use_blocks = slot_usable.reshape(capacity // count_len, count_len)

    def count_block(running, inputs):
        id_block, use_block = inputs
        matches = (id_block[None, :] == numbers[:, None]) & use_block[None, :]
        return (running + jnp.sum(matches.astype(jnp.float32), axis=1), None)

    local_counts, _ = lax.scan(
        count_block, jnp.zeros((local_windows,), jnp.float32), (id_blocks, use_blocks)
    )
    counts = lax.psum(local_counts, "frame")
    frame_devices = lax.axis_size("frame")
    row_count = capacity // frame_devices
    offsets = jnp.cumsum(lengths) - lengths
    own_offset = lax.dynamic_index_in_dim(offsets, my_index, keepdims=False)
    arranged = distances.reshape(restraints, row_count, frame_devices)
    rolled = jnp.roll(arranged, own_offset % frame_devices, axis=2)
    received = lax.all_to_all(rolled, "frame", split_axis=2, concat_axis=2, tiled=True)
    lead_slot = (my_index - offsets) % frame_devices
    delivered = jnp.maximum((lengths - lead_slot + frame_devices - 1) // frame_devices, 0)
    begin_at = jnp.cumsum(delivered) - delivered
    target = jnp.arange(BAL, dtype=jnp.int32)
    source = jnp.sum(((begin_at + delivered)[None, :] <= target[:, None]).astype(jnp.int32), axis=1)
    within = target - jnp.take(begin_at, source)
    received_flat = received.reshape(restraints, row_count * frame_devices)
    frames_here = jnp.take(received_flat, within * frame_devices + source, axis=1)
    usable = jnp.ones((BAL,), jnp.bool_)
    sampled = counts > 0.5
    log_count = jnp.log(jnp.maximum(counts, 1.0))
    slot_total = frames_here.shape[1]
    block_len = pick_block(slot_total)
    block_count = slot_total // block_len
    frame_blocks = frames_here.reshape(restraints, block_count, block_len).transpose(1, 0, 2)
    usable_blocks = usable.reshape(block_count, block_len)
    free_energy = jnp.zeros((local_windows,), jnp.float32)
    for iteration in range(ITERS):
        shifted = log_count + free_energy

        def den_block(separations):
            energy = energies(coef_rows, separations)
            exponent = jnp.where(sampled[:, None], shifted[:, None] - energy, floor_value)
            highest = jnp.max(exponent, axis=0)
            summed = jnp.sum(
                jnp.where(sampled[:, None], jnp.exp(exponent - highest[None, :]), 0.0), axis=0
            )
            return (highest, summed)

        highest, summed = lax.map(den_block, frame_blocks)
        log_den = denominators(highest.reshape(-1), summed.reshape(-1)).reshape(
            block_count, block_len
        )

        def frame_block(running, inputs):
            separations, den_values, use_block = inputs
            energy = energies(coef_rows, separations)
            exponent = jnp.where(use_block[None, :], -energy - den_values[None, :], floor_value)
            block_top = jnp.max(exponent, axis=1)
            block_sum = jnp.sum(
                jnp.where(use_block[None, :], jnp.exp(exponent - block_top[:, None]), 0.0), axis=1
            )
            return (pair_combine(running, (block_top, block_sum)), None)

        start_value = (
            jnp.full((local_windows,), floor_value, jnp.float32),
            jnp.zeros((local_windows,), jnp.float32),
        )
        running, _ = lax.scan(frame_block, start_value, (frame_blocks, log_den, usable_blocks))
        free_energy = window_totals(running[0], running[1])
    return free_energy


def solution(mesh):
    return jax.shard_map(
        on_device,
        mesh=mesh,
        in_specs=(P(None, "frame"), P("frame"), P(), P("win", None), P("win", None)),
        out_specs=P("win"),
        check_vma=False,
    )
```

profile of v0, /device:TPU:8, one launch (start us, length us, event | category | flops | bytes accessed | tf_op | source)
XLA Modules:
  0.0 833.9 jit_solution(18027603402774270897)
XLA Ops:
  0.0 0.7 copy.18
  0.9 0.7 fusion.21
  4.2 1.2 reshape.159
  5.8 0.9 copy.22
  6.7 1.2 reshape.445
  7.9 18.6 %all-to-all-start = ((f32[64,1,1024]{2,1,0:T(1,128)}), f32[64,1,1024]{2,1,0:T(1,128)S(1)}, u32[]{:S(2)}, u32[]{:S(2)}) async-start(f32[64,1,1024]{2,1,0:T(1,128)} %reshape.445), calls=%async_computation | async-start | bytes 524288 | tf_op jit(solution)/shard_map/all_to_all | solution.py:84
  26.4 0.6 dynamic_slice.40
  27.5 0.7 fusion.27
  28.2 0.7 fusion.26
  28.9 0.7 fusion.25
  29.6 0.7 fusion.24
  30.4 0.6 add_compare_fusion
  31.0 1.6 while.3
  32.6 143.2 %psum.35 = f32[512]{0:T(512)S(1)} all-reduce(f32[512]{0:T(512)S(1)} %get-tuple-element.89), channel_id=1, replica_groups=mesh['win'=8,'frame'=64] {'frame'}, use_global_device_ids=true, to_apply=%region_7.8 | all-reduce | flops 512 | bytes 4096 | tf_op jit(solution)/shard_map/psum | solution.py:77
  175.8 4.4 fusion.16
  180.2 0.9 compare_reduce_fusion.56
  181.1 35.6 %compare_and_fusion = (pred[1280]{0:T(1024)(128)(4,1)S(1)}, s32[1280]{0:T(1024)S(1)}) fusion(s32[1280]{0:T(1024)S(1)} %convert_reduce_fusion.1, pred[1280]{0:T(1024)(128)(4,1)S(1)} %get-tuple-element.188, pred[1280]{0:T(1024)(128)(4,1)S(1)} %get-tuple-element.186, pred[1280]{0:T(1024)(128)(4,1)S(1)} %get-tuple-element.187, ...), kind=kLoop, calls=%fused_computation.111 | loop fusion | flops 93440 | bytes 89828 | tf_op jit(solution)/shard_map/jit(_take)/and | solution.py:92
  217.5 1.3 reduce.122
  219.7 2.4 gather_fusion
  222.3 2.9 fusion.2
  225.2 10.3 %pmax.28 = f32[1280]{0:T(1024)S(1)} all-reduce(f32[1280]{0:T(1024)S(1)} %get-tuple-element.274), channel_id=1, replica_groups=mesh['win'=8,'frame'=64] {'win'}, use_global_device_ids=true, to_apply=%region_9.10 | all-reduce | flops 1280 | bytes 10240 | tf_op jit(solution)/shard_map/pmax | solution.py:43
  235.5 0.7 select_reduce_fusion.1
  236.2 12.9 %psum.36 = f32[1280]{0:T(1024)S(1)} all-reduce(f32[1280]{0:T(1024)S(1)} %exponential_multiply_fusion.1), channel_id=1, replica_groups=mesh['win'=8,'frame'=64] {'win'}, use_global_device_ids=true, to_apply=%region_11.12 | all-reduce | flops 1280 | bytes 10240 | tf_op jit(solution)/shard_map/psum | solution.py:44
  249.4 0.6 exponential_reduce_fusion.1
  250.1 138.0 %pmax.29 = f32[512]{0:T(512)S(1)} all-reduce(f32[512]{0:T(512)S(1)} %broadcast_maximum_fusion.1), channel_id=1, replica_groups=mesh['win'=8,'frame'=64] {'frame'}, use_global_device_ids=true, to_apply=%region_13.14 | all-reduce | flops 512 | bytes 4096 | tf_op jit(solution)/shard_map/pmax | solution.py:50
  388.1 139.9 %psum.37 = f32[512]{0:T(512)S(1)} all-reduce(f32[512]{0:T(512)S(1)} %exponential_multiply_fusion.3), channel_id=1, replica_groups=mesh['win'=8,'frame'=64] {'frame'}, use_global_device_ids=true, to_apply=%region_15.16 | all-reduce | flops 512 | bytes 4096 | tf_op jit(solution)/shard_map/psum | solution.py:51
  528.4 0.7 select_reduce_fusion
  529.1 12.0 %pmax.30 = f32[1280]{0:T(1024)S(1)} all-reduce(f32[1280]{0:T(1024)S(1)} %fusion.3), channel_id=1, replica_groups=mesh['win'=8,'frame'=64] {'win'}, use_global_device_ids=true, to_apply=%region_17.18 | all-reduce | flops 1280 | bytes 10240 | tf_op jit(solution)/shard_map/pmax | solution.py:43
  541.2 13.2 %psum.38 = f32[1280]{0:T(1024)S(1)} all-reduce(f32[1280]{0:T(1024)S(1)} %exponential_multiply_fusion), channel_id=1, replica_groups=mesh['win'=8,'frame'=64] {'win'}, use_global_device_ids=true, to_apply=%region_19.20 | all-reduce | flops 1280 | bytes 10240 | tf_op jit(solution)/shard_map/psum | solution.py:44
  554.7 0.6 exponential_reduce_fusion
  555.4 138.0 %pmax.31 = f32[512]{0:T(512)S(1)} all-reduce(f32[512]{0:T(512)S(1)} %broadcast_maximum_fusion), channel_id=1, replica_groups=mesh['win'=8,'frame'=64] {'frame'}, use_global_device_ids=true, to_apply=%region_21.22 | all-reduce | flops 512 | bytes 4096 | tf_op jit(solution)/shard_map/pmax | solution.py:50
  693.4 140.0 %psum.39 = f32[512]{0:T(512)S(1)} all-reduce(f32[512]{0:T(512)S(1)} %exponential_multiply_fusion.2), channel_id=1, replica_groups=mesh['win'=8,'frame'=64] {'frame'}, use_global_device_ids=true, to_apply=%region_23.24 | all-reduce | flops 512 | bytes 4096 | tf_op jit(solution)/shard_map/psum | solution.py:51
  (63 shorter events, 6.5 us)
Async XLA Ops:
  4.2 22.2 %copy-start.3 = (s32[64]{0:T(128)S(1)}, s32[64]{0:T(128)}, u32[]{:S(2)}) copy-start(s32[64]{0:T(128)} %param.9) | copy-start | bytes 772
  4.2 26.8 %copy-start.2 = (s32[2048]{0:T(1024)S(1)}, s32[2048]{0:T(1024)}, u32[]{:S(2)}) copy-start(s32[2048]{0:T(1024)} %param.8) | copy-start | bytes 24580
  5.4 211.5 %copy-start = (f32[512,32]{0,1:T(8,128)S(1)}, f32[512,32]{0,1:T(8,128)}, u32[]{:S(2)}) copy-start(f32[512,32]{0,1:T(8,128)} %param.11) | copy-start | bytes 196612
  5.4 211.5 %copy-start.1 = (f32[512,32]{0,1:T(8,128)S(1)}, f32[512,32]{0,1:T(8,128)}, u32[]{:S(2)}) copy-start(f32[512,32]{0,1:T(8,128)} %param.10) | copy-start | bytes 196612
  7.9 209.1 %all-to-all-start = ((f32[64,1,1024]{2,1,0:T(1,128)}), f32[64,1,1024]{2,1,0:T(1,128)S(1)}, u32[]{:S(2)}, u32[]{:S(2)}) async-start(f32[64,1,1024]{2,1,0:T(1,128)} %reshape.445), calls=%async_computation | async-start | bytes 524288 | tf_op jit(solution)/shard_map/all_to_all | solution.py:84
where the time goes:
time: 836 us; the launch traced here: 834 us
  blocking collectives  747 us (89%)
  other arithmetic  50.4 us (6%)
  starting transfers between devices  18.6 us (2%)
  local copies, waits for them, and re-layouts  12.1 us (1%)
    psum x2, blocking collectives, window_totals(): summed = lax.psum(summed * jnp.exp(highest - global_top), 'frame')  280 us
    pmax x2, blocking collectives, window_totals(): global_top = lax.pmax(highest, 'frame')  276 us
    psum x1, blocking collectives, on_device(): counts = lax.psum(local_counts, 'frame')  143 us
    and x1, other arithmetic, on_device(): jnp.take(received_flat, within * frame_devices + source, axis=1)  35.6 us
    psum x2, blocking collectives, denominators(): summed = lax.psum(summed * jnp.exp(highest - global_top), 'win')  26.1 us
    pmax x2, blocking collectives, denominators(): global_top = lax.pmax(highest, 'win')  22.3 us
    all_to_all x1, starting transfers between devices, on_device(): lax.all_to_all(rolled, 'frame', split_axis=2, concat_axis=2, tiled=True)  18.6 us
  transfers between devices with their start and end apart: 1, of which 0 were waited for; matrix products, arithmetic and copies ran while one was open for 6% of the time, Pallas kernels for 0%

commit v1 on v0

v1 whole, which is shorter than its diff:
```python
import jax
import jax.numpy as jnp
from jax import lax
from jax.sharding import PartitionSpec as P

ITERS = 2


floor_value = -1e30


def coefficients(stiffness, centers):
    constant = jnp.sum(0.5 * stiffness * centers * centers, axis=1, keepdims=True)
    return jnp.concatenate([constant, -stiffness * centers, 0.5 * stiffness], axis=1)


def features(separations):
    unit_row = jnp.ones((1, separations.shape[1]), separations.dtype)
    return jnp.concatenate([unit_row, separations, separations * separations], axis=0)


def energies(coef_rows, separations):
    return jnp.dot(
        coef_rows,
        features(separations),
        precision=lax.Precision.HIGHEST,
        preferred_element_type=jnp.float32,
    )


def share(values, axis):
    copies = jnp.broadcast_to(values[None, :], (lax.axis_size(axis), values.shape[0]))
    return lax.all_to_all(copies, axis, split_axis=0, concat_axis=0, tiled=True)


def log_sum_exp(values, axis):
    highest = jnp.max(values, axis=axis, keepdims=True)
    return jnp.squeeze(highest, axis) + jnp.log(jnp.sum(jnp.exp(values - highest), axis=axis))


def on_device(distances, sample_ids, lengths, stiffness, centers):
    local_windows = stiffness.shape[0]
    capacity = distances.shape[1]
    own_length = lax.dynamic_index_in_dim(lengths, lax.axis_index("frame"), keepdims=False)
    slot_usable = jnp.arange(capacity, dtype=jnp.int32) < own_length
    numbers = lax.axis_index("win") * local_windows + jnp.arange(local_windows, dtype=jnp.int32)
    ids = jnp.where(slot_usable, sample_ids, -1)
    local_counts = jnp.sum((ids[None, :] == numbers[:, None]).astype(jnp.float32), axis=1)
    counts = jnp.sum(share(local_counts, "frame"), axis=0)
    energy = energies(coefficients(stiffness, centers), distances)
    sampled = counts > 0.5
    log_count = jnp.log(jnp.maximum(counts, 1.0))
    free_energy = jnp.zeros((local_windows,), jnp.float32)
    for iteration in range(ITERS):
        shifted = jnp.where(sampled, log_count + free_energy, floor_value)
        own_den = log_sum_exp(shifted[:, None] - energy, 0)
        log_den = log_sum_exp(share(own_den, "win"), 0)
        log_den = jnp.where(slot_usable, log_den, -floor_value)
        own_total = log_sum_exp(-energy - log_den[None, :], 1)
        free_energy = -log_sum_exp(share(own_total, "frame"), 0)
    return free_energy


def solution(mesh):
    return jax.shard_map(
        on_device,
        mesh=mesh,
        in_specs=(P(None, "frame"), P("frame"), P(), P("win", None), P("win", None)),
        out_specs=P("win"),
        check_vma=False,
    )
```

time: 836 us -> 123 us (0.15)
  the two profiles are of different devices: /device:TPU:8 before, /device:TPU:1 now
where the time goes in v1:
time: 123 us; the launch traced here: 122 us
  blocking collectives  61.6 us (50%)
  starting transfers between devices  19.1 us (16%)
  other arithmetic  18.7 us (15%)
  waiting for transfers between devices  12.9 us (10%)
  local copies, waits for them, and re-layouts  4.8 us (4%)
  matrix products  4.68 us (4%)
    all_to_all x4, blocking collectives, share(): return lax.all_to_all(copies, axis, split_axis=0, concat_axis=0, tiled=True)  61.6 us
    all_to_all x1, starting transfers between devices, share(): return lax.all_to_all(copies, axis, split_axis=0, concat_axis=0, tiled=True)  19.1 us
    all_to_all x1, waiting for transfers between devices, share(): return lax.all_to_all(copies, axis, split_axis=0, concat_axis=0, tiled=True)  12.9 us
    reduce_max x7, other arithmetic, log_sum_exp(): highest = jnp.max(values, axis=axis, keepdims=True)  8.81 us
    dot_general x1, matrix products, energies(): jnp.dot(coef_rows, features(separations), precision=lax.Precision.HIGHEST...  4.68 us
    reduce_sum x8, other arithmetic, log_sum_exp(): jnp.sum(jnp.exp(values - highest), axis=axis)  3.57 us
    unnamed x8, local copies, waits for them, and re-layouts  2.62 us
  transfers between devices with their start and end apart: 1, of which 1 were waited for; matrix products, arithmetic and copies ran while one was open for 2% of the time, Pallas kernels for 0%

profile of v1, /device:TPU:1, one launch (start us, length us, event | category | flops | bytes accessed | tf_op | source)
XLA Modules:
  0.0 122.0 jit_solution(15152837524458096067)
XLA Ops:
  0.0 1.2 %dynamic_slice.4 = s32[1]{0:T(128)} dynamic-slice(s32[64]{0:T(128)} %param.7, s32[]{:T(128)S(6)} %select_n.38), dynamic_slice_sizes={1} | dynamic-slice | bytes 12 | tf_op jit(solution)/shard_map/jit(dynamic_index_in_dim)/dynamic_slice | solution.py:44
  1.2 1.3 %fusion.20 = s32[2048]{0:T(1024)S(1)} fusion(s32[2048]{0:T(1024)} %param.6, s32[]{:T(128)} %bitcast.1), kind=kLoop, calls=%fused_computation.41 | loop fusion | flops 4096 | bytes 16388 | tf_op jit(solution)/shard_map/jit(_where)/select_n | solution.py:47
  2.6 0.5 convert_reduce_fusion
  3.1 0.7 broadcast_in_dim.31
  3.9 19.1 %all-to-all-start = ((f32[64,1,512]{2,1,0:T(1,128)}), f32[64,1,512]{2,1,0:T(1,128)S(1)}, u32[]{:S(2)}, u32[]{:S(2)}) async-start(f32[64,1,512]{2,1,0:T(1,128)} %broadcast_in_dim.31), calls=%async_computation | async-start | bytes 262144 | tf_op jit(solution)/shard_map/all_to_all | solution.py:33
  23.0 1.1 mul.23
  24.1 0.9 fusion.15
  25.0 12.9 %all-to-all-done = f32[64,1,512]{2,1,0:T(1,128)S(1)} async-done(((f32[64,1,512]{2,1,0:T(1,128)}), f32[64,1,512]{2,1,0:T(1,128)S(1)}, u32[]{:S(2)}, u32[]{:S(2)}) %all-to-all-start) | async-done | bytes 131104 | tf_op jit(solution)/shard_map/all_to_all | solution.py:33
  37.9 0.1 reduce_sum.101
  38.0 4.7 %subtract_reduce_fusion.3 = (f32[2048]{0:T(1024)S(1)}, f32[512,2048]{1,0:T(8,128)S(1)}) fusion(f32[512]{0:T(512)S(1)} %fusion.21, f32[32,2048]{1,0:T(8,128)S(1)} %mul.23, f32[32,2048]{1,0:T(8,128)} %param.5, f32[65]{0:T(128)S(1)} %pad.clone, f32[512,32]{0,1:T(8,128)S(1)} %get-tuple-element.7, f32[512,32]{0,1:T(8,128)S(1)} %get-tuple-element.6, ...), kind=kOutput, calls=%fused_computation.8 | convolution fusion | flops 820317184 | bytes 4862212 | tf_op jit(solution)/shard_map/dot_general | solution.py:23
  42.7 1.9 %copy-done = f32[512,2048]{1,0:T(8,128)} copy-done((f32[512,2048]{1,0:T(8,128)}, f32[512,2048]{1,0:T(8,128)S(1)}, u32[]{:S(2)}) %copy-start) | copy-done | bytes 4194328
  44.6 0.8 exponential_reduce_fusion.3
  45.5 12.8 %all_to_all.42 = f32[8,1,2048]{2,1,0:T(1,128)S(1)} all-to-all(f32[8,1,2048]{2,1,0:T(1,128)S(1)} %broadcast_in_dim.33), channel_id=1, replica_groups=mesh['win'=8,'frame'=64] {'win'}, dimensions={0} | all-to-all | bytes 131072 | tf_op jit(solution)/shard_map/all_to_all | solution.py:33
  58.3 0.1 reduce_max.73
  58.4 0.8 add_select_fusion.1
  59.2 2.9 %subtract_reduce_fusion.2 = f32[512]{0:T(512)S(1)} fusion(f32[512,2048]{1,0:T(8,128)} %copy-done, f32[2048]{0:T(1024)S(1)} %add_select_fusion.1), kind=kLoop, calls=%fused_computation.7 | loop fusion | flops 3145216 | bytes 4204544 | tf_op jit(solution)/shard_map/reduce_max | solution.py:37
  62.1 0.9 exponential_reduce_fusion.2
  63.1 0.1 broadcast_in_dim.35
  63.2 19.1 %all_to_all.43 = f32[64,1,512]{2,1,0:T(1,128)S(1)} all-to-all(f32[64,1,512]{2,1,0:T(1,128)S(1)} %broadcast_in_dim.35), channel_id=1, replica_groups=mesh['win'=8,'frame'=64] {'frame'}, dimensions={0} | all-to-all | bytes 262144 | tf_op jit(solution)/shard_map/all_to_all | solution.py:33
  82.3 0.1 reduce_max.75
  82.4 2.7 %subtract_reduce_fusion.1 = f32[2048]{0:T(1024)S(1)} fusion(f32[512,2048]{1,0:T(8,128)} %copy-done, f32[512]{0:T(512)S(1)} %add_select_fusion.2), kind=kLoop, calls=%fused_computation.6 | loop fusion | flops 2095104 | bytes 4204544 | tf_op jit(solution)/shard_map/reduce_max | solution.py:37
  85.1 0.7 copy-done.2
  85.8 0.8 exponential_reduce_fusion.1
  86.7 10.6 %all_to_all.44 = f32[8,1,2048]{2,1,0:T(1,128)S(1)} all-to-all(f32[8,1,2048]{2,1,0:T(1,128)S(1)} %broadcast_in_dim.36), channel_id=1, replica_groups=mesh['win'=8,'frame'=64] {'win'}, dimensions={0} | all-to-all | bytes 131072 | tf_op jit(solution)/shard_map/all_to_all | solution.py:33
  97.3 0.1 reduce_max.77
  97.4 0.8 add_select_fusion
  98.2 2.9 %subtract_reduce_fusion = f32[512]{0:T(512)S(1)} fusion(f32[512,2048]{1,0:T(8,128)} %copy-done, f32[2048]{0:T(1024)S(1)} %add_select_fusion), kind=kLoop, calls=%fused_computation.5 | loop fusion | flops 3145216 | bytes 4204544 | tf_op jit(solution)/shard_map/reduce_max | solution.py:37
  101.1 0.9 exponential_reduce_fusion
  102.1 0.1 broadcast_in_dim.37
  102.1 19.1 %all_to_all.45 = f32[64,1,512]{2,1,0:T(1,128)S(1)} all-to-all(f32[64,1,512]{2,1,0:T(1,128)S(1)} %broadcast_in_dim.37), channel_id=1, replica_groups=mesh['win'=8,'frame'=64] {'frame'}, dimensions={0} | all-to-all | bytes 262144 | tf_op jit(solution)/shard_map/all_to_all | solution.py:33
  121.2 0.1 reduce_max.79
  121.4 0.6 add_negate_fusion
  (20 shorter events, 0.3 us)
Async XLA Ops:
  3.9 34.0 %all-to-all-start = ((f32[64,1,512]{2,1,0:T(1,128)}), f32[64,1,512]{2,1,0:T(1,128)S(1)}, u32[]{:S(2)}, u32[]{:S(2)}) async-start(f32[64,1,512]{2,1,0:T(1,128)} %broadcast_in_dim.31), calls=%async_computation | async-start | bytes 262144 | tf_op jit(solution)/shard_map/all_to_all | solution.py:33
  42.7 1.9 %copy-start = (f32[512,2048]{1,0:T(8,128)}, f32[512,2048]{1,0:T(8,128)S(1)}, u32[]{:S(2)}) copy-start(f32[512,2048]{1,0:T(8,128)S(1)} %get-tuple-element.9) | copy-start | bytes 12582916
  58.4 3.8 %copy-start.1 = (f32[512,2048]{1,0:T(8,128)S(1)}, f32[512,2048]{1,0:T(8,128)}, u32[]{:S(2)}) copy-start(f32[512,2048]{1,0:T(8,128)} %copy-done) | copy-start | bytes 12582916
  82.4 3.4 %copy-start.2 = (f32[512,2048]{1,0:T(8,128)S(1)}, f32[512,2048]{1,0:T(8,128)}, u32[]{:S(2)}) copy-start(f32[512,2048]{1,0:T(8,128)} %copy-done) | copy-start | bytes 12582916
  97.3 3.8 %copy-start.3 = (f32[512,2048]{1,0:T(8,128)S(1)}, f32[512,2048]{1,0:T(8,128)}, u32[]{:S(2)}) copy-start(f32[512,2048]{1,0:T(8,128)} %copy-done) | copy-start | bytes 12582916

commit v2 on v1

v2 whole, which is shorter than its diff:
```python
import functools

import jax
import jax.numpy as jnp
from jax import lax
from jax.experimental import pallas as pl
from jax.experimental.pallas import tpu as pltpu
from jax.sharding import PartitionSpec as P

ITERS = 2
LANES = 128
ROWS = 64

floor_value = -1e30

in_vmem = pl.BlockSpec(memory_space=pltpu.VMEM)
in_smem = pl.BlockSpec(memory_space=pltpu.SMEM)
small_grant = pltpu.CompilerParams(vmem_limit_bytes=12 << 20)


def log_sum_exp(values):
    highest = jnp.max(values, axis=0)
    return highest + jnp.log(jnp.sum(jnp.exp(values - highest[None]), axis=0))


def count_kernel(lengths_ref, ids_ref, out_ref):
    groups = out_ref.shape[1]
    capacity = ids_ref.shape[1]
    own_length = lengths_ref[lax.axis_index("frame")]
    local = ids_ref[...] - lax.axis_index("win") * (groups * LANES)
    slots = lax.broadcasted_iota(jnp.int32, (1, capacity), 1)
    local = jnp.where(slots < own_length, local, -1)
    group = jnp.where(local < 0, -1, lax.shift_right_logical(local, 7))
    place = jnp.bitwise_and(local, LANES - 1)
    in_group = lax.broadcasted_iota(jnp.int32, (8, capacity), 0) == group
    in_place = lax.broadcasted_iota(jnp.int32, (LANES, capacity), 0) == place
    counts = lax.dot_general(
        in_group.astype(jnp.float32).astype(jnp.bfloat16),
        in_place.astype(jnp.float32).astype(jnp.bfloat16),
        (((1,), (1,)), ((), ())),
        preferred_element_type=jnp.float32,
    )
    out_ref[...] = jnp.broadcast_to(counts[None, :groups], out_ref.shape)


def energy_kernel(stiffness_ref, centers_ref, distances_ref, energy_ref):
    stiffness, centers = stiffness_ref[...], centers_ref[...]
    constant = jnp.sum(0.5 * stiffness * centers * centers, axis=0, keepdims=True)
    first = lax.broadcasted_iota(jnp.int32, (8, constant.shape[1]), 0) == 0
    constant_rows = jnp.where(first, jnp.broadcast_to(constant, first.shape), 0.0)
    coef_rows = jnp.concatenate([-stiffness * centers, 0.5 * stiffness, constant_rows], axis=0).T
    step = 512
    unit_rows = jnp.where(lax.broadcasted_iota(jnp.int32, (8, step), 0) == 0, 1.0, 0.0)

    def one(block, carry):
        columns = pl.ds(pl.multiple_of(block * step, step), step)
        separations = distances_ref[:, columns]
        features = jnp.concatenate([separations, separations * separations, unit_rows], axis=0)
        energy_ref[:, columns] = jnp.dot(
            coef_rows, features, precision=lax.Precision.HIGHEST, preferred_element_type=jnp.float32
        )
        return carry

    lax.fori_loop(0, distances_ref.shape[1] // step, one, 0)


def denominators(shifted, energy_ref, out_ref, column_ref, row_ref):
    groups = shifted.shape[0]
    for group in range(groups):
        spread = jnp.broadcast_to(shifted[group : group + 1], (LANES, LANES))
        column_ref[group * LANES : (group + 1) * LANES, :] = spread.T
    windows = column_ref.shape[0]
    chunks = [slice(start, start + ROWS) for start in range(0, windows, ROWS)]

    def one(block, carry):
        columns = pl.ds(pl.multiple_of(block * LANES, LANES), LANES)
        tops = [
            jnp.max((column_ref[rows, :] - energy_ref[rows, columns]).reshape(-1, 8, LANES), axis=0)
            for rows in chunks
        ]
        highest = jnp.max(functools.reduce(jnp.maximum, tops), axis=0, keepdims=True)
        sums = [
            jnp.sum(
                jnp.exp(column_ref[rows, :] - energy_ref[rows, columns] - highest).reshape(-1, 8, LANES),
                axis=0,
            )
            for rows in chunks
        ]
        total = jnp.sum(functools.reduce(jnp.add, sums), axis=0, keepdims=True)
        row_ref[pl.ds(block, 1), :] = highest + jnp.log(total)
        return carry

    lax.fori_loop(0, energy_ref.shape[1] // LANES, one, 0, unroll=2)
    out_ref[...] = jnp.broadcast_to(row_ref[...][None], out_ref.shape)


def first_kernel(shared_ref, energy_ref, counts_ref, out_ref, column_ref, row_ref):
    counts = jnp.sum(shared_ref[...], axis=0)
    counts_ref[...] = counts
    shifted = jnp.where(counts > 0.5, jnp.log(jnp.maximum(counts, 1.0)), floor_value)
    denominators(shifted, energy_ref, out_ref, column_ref, row_ref)


def next_kernel(shared_ref, counts_ref, energy_ref, out_ref, column_ref, row_ref):
    counts = counts_ref[...]
    free_energy = -log_sum_exp(shared_ref[...])
    shifted = jnp.where(counts > 0.5, jnp.log(jnp.maximum(counts, 1.0)) + free_energy, floor_value)
    denominators(shifted, energy_ref, out_ref, column_ref, row_ref)


def window_kernel(lengths_ref, shared_ref, energy_ref, out_ref, den_ref, top_ref, sum_ref):
    own_length = lengths_ref[lax.axis_index("frame")]
    blocks, windows = shared_ref.shape[1], energy_ref.shape[0]
    log_den = log_sum_exp(shared_ref[...])
    slots = (
        lax.broadcasted_iota(jnp.int32, (blocks, LANES), 0) * LANES
        + lax.broadcasted_iota(jnp.int32, (blocks, LANES), 1)
    )
    den_ref[...] = jnp.where(slots < own_length, log_den, -floor_value)

    def one(chunk, carry):
        rows = pl.ds(pl.multiple_of(chunk * ROWS, ROWS), ROWS)
        top = jnp.full((ROWS, LANES), 2.0 * floor_value, jnp.float32)
        for block in range(blocks):
            columns = slice(block * LANES, (block + 1) * LANES)
            top = jnp.maximum(top, -energy_ref[rows, columns] - den_ref[block : block + 1, :])
        total = jnp.zeros((ROWS, LANES), jnp.float32)
        for block in range(blocks):
            columns = slice(block * LANES, (block + 1) * LANES)
            total = total + jnp.exp(-energy_ref[rows, columns] - den_ref[block : block + 1, :] - top)
        top_ref[rows, :] = top
        sum_ref[rows, :] = total
        return carry

    lax.fori_loop(0, windows // ROWS, one, 0)
    for group in range(windows // LANES):
        rows = slice(group * LANES, (group + 1) * LANES)
        tops, sums = top_ref[rows, :].T, sum_ref[rows, :].T
        highest = jnp.max(tops, axis=0, keepdims=True)
        total = jnp.sum(sums * jnp.exp(tops - highest), axis=0, keepdims=True)
        row = highest + jnp.log(total)
        out_ref[:, group : group + 1, :] = jnp.broadcast_to(row[None], (out_ref.shape[0], 1, LANES))


def exchange(copies, axis):
    return lax.all_to_all(copies, axis, split_axis=0, concat_axis=0, tiled=True)


def on_device(distances, sample_ids, lengths, stiffness, centers):
    windows, capacity = stiffness.shape[0], distances.shape[1]
    groups, blocks = windows // LANES, capacity // LANES
    frame_devices, win_devices = lax.axis_size("frame"), lax.axis_size("win")
    f32 = jnp.float32
    to_frame = jax.ShapeDtypeStruct((frame_devices, groups, LANES), f32)
    to_win = jax.ShapeDtypeStruct((win_devices, blocks, LANES), f32)
    energy_cost = pl.CostEstimate(
        flops=12 * 2 * distances.shape[0] * windows * capacity, bytes_accessed=4 * windows * capacity, transcendentals=0
    )
    local_counts = pl.pallas_call(
        count_kernel, out_shape=to_frame, in_specs=[in_smem, in_vmem], out_specs=in_vmem, compiler_params=small_grant, name="count_windows"
    )(lengths, sample_ids.reshape(1, capacity))
    shared = exchange(local_counts, "frame")
    energy = pl.pallas_call(
        energy_kernel,
        out_shape=jax.ShapeDtypeStruct((windows, capacity), f32),
        in_specs=[in_vmem] * 3,
        out_specs=in_vmem,
        cost_estimate=energy_cost,
        compiler_params=small_grant,
        name="energies",
    )(stiffness.T, centers.T, distances)
    scratch = [pltpu.VMEM((windows, LANES), f32), pltpu.VMEM((blocks, LANES), f32)]
    counts, own_den = pl.pallas_call(
        first_kernel,
        out_shape=(jax.ShapeDtypeStruct((groups, LANES), f32), to_win),
        in_specs=[in_vmem] * 2,
        out_specs=(in_vmem, in_vmem),
        scratch_shapes=scratch,
        compiler_params=small_grant,
        name="first_denominators",
    )(shared, energy)
    for iteration in range(ITERS):
        own_total = pl.pallas_call(
            window_kernel,
            out_shape=to_frame,
            in_specs=[in_smem, in_vmem, in_vmem],
            out_specs=in_vmem,
            scratch_shapes=[pltpu.VMEM((blocks, LANES), f32)] + [pltpu.VMEM((windows, LANES), f32)] * 2,
            compiler_params=small_grant,
            name="window_totals",
        )(lengths, exchange(own_den, "win"), energy)
        shared = exchange(own_total, "frame")
        if iteration < ITERS - 1:
            own_den = pl.pallas_call(
                next_kernel,
                out_shape=to_win,
                in_specs=[in_vmem] * 3,
                out_specs=in_vmem,
                scratch_shapes=scratch,
                compiler_params=small_grant,
                name="next_denominators",
            )(shared, counts, energy)
    return -log_sum_exp(shared).reshape(windows)


def solution(mesh):
    return jax.shard_map(
        on_device,
        mesh=mesh,
        in_specs=(P(None, "frame"), P("frame"), P(), P("win", None), P("win", None)),
        out_specs=P("win"),
        check_vma=False,
    )
```

time: 123 us -> 112 us (0.911)
  other arithmetic: 18.7 us -> 0.76 us
  Pallas kernels: 0 us -> 13 us
  waiting for transfers between devices: 12.9 us -> 6.33 us
  matrix products: 4.68 us -> 0 us
  local copies, waits for them, and re-layouts: 4.8 us -> 8.11 us
  blocking collectives: 61.6 us -> 63.3 us
    pallas_call x0 -> x6, Pallas kernels: none -> 13 us  [the longest x2 4.05 us: on_device(): pl.pallas_call(window_kernel, out_shape=to_frame, in_specs=[in_smem, in_v...]
    reduce_max x7 -> x1, other arithmetic: 8.81 us -> 0.08 us  [log_sum_exp(): highest = jnp.max(values, axis=0)]
    all_to_all x1, waiting for transfers between devices: 12.9 us -> 6.33 us  [exchange(): return lax.all_to_all(copies, axis, split_axis=0, concat_axis=0, tiled=True)]
    unnamed x8 -> x18, local copies, waits for them, and re-layouts: 2.62 us -> 8.11 us
    reduce_sum x11 -> x1, other arithmetic: 5.14 us -> 0.09 us  [log_sum_exp(): return highest + jnp.log(jnp.sum(jnp.exp(values - highest[None]), axis=0))]
    dot_general x1 -> x0, matrix products: 4.68 us -> none  [energies(): jnp.dot(coef_rows, features(separations), precision=lax.Precision.HIGHEST...]
    select_n x5 -> x0, other arithmetic: 2.97 us -> none  [the longest x2 1.61 us: on_device(): log_den = jnp.where(slot_usable, log_den, -floor_value)]
    all_to_all x4, blocking collectives: 61.6 us -> 63.3 us  [exchange(): return lax.all_to_all(copies, axis, split_axis=0, concat_axis=0, tiled=True)]
  transfers between devices with their start and end apart: 1 -> 1, of which waited for: 1 -> 1; matrix products, arithmetic and copies ran while one was open for 2% -> 0% of each run, Pallas kernels for 0% -> 4%
where the time goes in v2:
time: 112 us; the launch traced here: 111 us
  blocking collectives  63.3 us (57%)
  starting transfers between devices  19.1 us (17%)
  Pallas kernels  13 us (12%)
  local copies, waits for them, and re-layouts  8.11 us (7%)
  waiting for transfers between devices  6.33 us (6%)
    all_to_all x4, blocking collectives, exchange(): return lax.all_to_all(copies, axis, split_axis=0, concat_axis=0, tiled=True)  63.3 us
    all_to_all x1, starting transfers between devices, exchange(): return lax.all_to_all(copies, axis, split_axis=0, concat_axis=0, tiled=True)  19.1 us
    unnamed x18, local copies, waits for them, and re-layouts  8.11 us
    all_to_all x1, waiting for transfers between devices, exchange(): return lax.all_to_all(copies, axis, split_axis=0, concat_axis=0, tiled=True)  6.33 us
    pallas_call x2, Pallas kernels, on_device(): pl.pallas_call(window_kernel, out_shape=to_frame, in_specs=[in_smem, in_v...  4.05 us
    pallas_call x1, Pallas kernels, on_device(): pl.pallas_call(energy_kernel, out_shape=jax.ShapeDtypeStruct((windows, ca...  3.98 us
  transfers between devices with their start and end apart: 1, of which 1 were waited for; matrix products, arithmetic and copies ran while one was open for 0% of the time, Pallas kernels for 4%

profile of v2, /device:TPU:1, one launch (start us, length us, event | category | flops | bytes accessed | tf_op | source)
XLA Modules:
  0.0 110.7 jit_solution(14333706664332067167)
XLA Ops:
  0.0 0.0 copy-start.6
  0.0 0.7 copy-done.6
  0.7 0.0 copy-start.7
  0.7 0.7 copy-done.7
  1.4 1.5 %count_windows.1 = f32[64,4,128]{2,1,0:T(4,128)} custom-call(s32[64]{0:T(128)S(1)} %copy-done.7, s32[1,2048]{1,0:T(1,128)S(1)} %bitcast.7), custom_call_target="tpu_custom_call" | custom-call | tf_op jit(solution)/shard_map/count_windows/pallas_call | solution.py:159
  2.8 19.1 %all-to-all-start = ((f32[64,4,128]{2,1,0:T(4,128)}), f32[64,4,128]{2,1,0:T(4,128)S(1)}, u32[]{:S(2)}, u32[]{:S(2)}) async-start(f32[64,4,128]{2,1,0:T(4,128)} %count_windows.1), calls=%async_computation | async-start | bytes 262144 | tf_op jit(solution)/shard_map/all_to_all | solution.py:146
  21.9 0.0 copy-start.3
  22.0 0.9 copy-done.3
  22.9 0.0 copy-start.4
  22.9 0.8 copy-done.4
  23.7 0.0 copy-start.5
  23.7 0.8 copy-done.5
  24.6 0.0 copy-start.8
  24.6 4.0 %energies.1.energy_ref = f32[512,2048]{1,0:T(8,128)S(1)} custom-call(f32[32,512]{1,0:T(8,128)S(1)} %bitcast.5, f32[32,512]{1,0:T(8,128)S(1)} %bitcast.6, f32[32,2048]{1,0:T(8,128)S(1)} %copy-done.3), custom_call_target="tpu_custom_call" | custom-call | flops 805306368 | bytes 4194304 | tf_op jit(solution)/shard_map/energies/pallas_call | solution.py:163
  28.6 0.0 copy-start
  28.6 1.9 %copy-done = f32[512,2048]{1,0:T(8,128)} copy-done((f32[512,2048]{1,0:T(8,128)}, f32[512,2048]{1,0:T(8,128)S(1)}, u32[]{:S(2)}) %copy-start) | copy-done | bytes 4194328
  30.5 6.3 %all-to-all-done.shared_ref = f32[64,4,128]{2,1,0:T(4,128)S(1)} async-done(((f32[64,4,128]{2,1,0:T(4,128)}), f32[64,4,128]{2,1,0:T(4,128)S(1)}, u32[]{:S(2)}, u32[]{:S(2)}) %all-to-all-start) | async-done | bytes 131104 | tf_op jit(solution)/shard_map/all_to_all | solution.py:146
  36.8 0.0 copy-start.1
  36.8 2.2 %copy-done.1 = f32[512,2048]{1,0:T(8,128)S(1)} copy-done((f32[512,2048]{1,0:T(8,128)S(1)}, f32[512,2048]{1,0:T(8,128)}, u32[]{:S(2)}) %copy-start.1) | copy-done | bytes 4194328
  39.0 1.7 %first_denominators.1 = (f32[4,128]{1,0:T(4,128)S(1)}, f32[8,16,128]{2,1,0:T(8,128)S(1)}) custom-call(f32[64,4,128]{2,1,0:T(4,128)S(1)} %all-to-all-done.shared_ref, f32[512,2048]{1,0:T(8,128)S(1)} %copy-done.1), custom_call_target="tpu_custom_call" | custom-call | tf_op jit(solution)/shard_map/first_denominators/pallas_call | solution.py:173
  40.8 12.8 %all_to_all.25.shared_ref = f32[8,16,128]{2,1,0:T(8,128)S(1)} all-to-all(f32[8,16,128]{2,1,0:T(8,128)S(1)} %get-tuple-element.7), channel_id=1, replica_groups=mesh['win'=8,'frame'=64] {'win'}, dimensions={0} | all-to-all | bytes 131072 | tf_op jit(solution)/shard_map/all_to_all | solution.py:146
  53.6 0.0 copy-done.8
  53.6 0.0 copy-done.2
  53.6 2.0 %window_totals.2 = f32[64,4,128]{2,1,0:T(4,128)S(1)} custom-call(s32[64]{0:T(128)S(1)} %copy-done.8, f32[8,16,128]{2,1,0:T(8,128)S(1)} %all_to_all.25.shared_ref, f32[512,2048]{1,0:T(8,128)S(1)} %copy-done.2), custom_call_target="tpu_custom_call" | custom-call | tf_op jit(solution)/shard_map/window_totals/pallas_call | solution.py:183
  55.6 20.5 %all_to_all.26.shared_ref = f32[64,4,128]{2,1,0:T(4,128)S(1)} all-to-all(f32[64,4,128]{2,1,0:T(4,128)S(1)} %window_totals.2), channel_id=1, replica_groups=mesh['win'=8,'frame'=64] {'frame'}, dimensions={0} | all-to-all | bytes 262144 | tf_op jit(solution)/shard_map/all_to_all | solution.py:146
  76.2 1.8 %next_denominators.1 = f32[8,16,128]{2,1,0:T(8,128)S(1)} custom-call(f32[64,4,128]{2,1,0:T(4,128)S(1)} %all_to_all.26.shared_ref, f32[4,128]{1,0:T(4,128)S(1)} %get-tuple-element.8.counts_ref, f32[512,2048]{1,0:T(8,128)S(1)} %copy-done.2), custom_call_target="tpu_custom_call" | custom-call | tf_op jit(solution)/shard_map/next_denominators/pallas_call | solution.py:194
  77.9 10.8 %all_to_all.27.shared_ref = f32[8,16,128]{2,1,0:T(8,128)S(1)} all-to-all(f32[8,16,128]{2,1,0:T(8,128)S(1)} %next_denominators.1), channel_id=1, replica_groups=mesh['win'=8,'frame'=64] {'win'}, dimensions={0} | all-to-all | bytes 131072 | tf_op jit(solution)/shard_map/all_to_all | solution.py:146
  88.8 2.0 %window_totals.3 = f32[64,4,128]{2,1,0:T(4,128)S(1)} custom-call(s32[64]{0:T(128)S(1)} %copy-done.8, f32[8,16,128]{2,1,0:T(8,128)S(1)} %all_to_all.27.shared_ref, f32[512,2048]{1,0:T(8,128)S(1)} %copy-done.2), custom_call_target="tpu_custom_call" | custom-call | tf_op jit(solution)/shard_map/window_totals/pallas_call | solution.py:183
  90.8 19.1 %all_to_all.28 = f32[64,4,128]{2,1,0:T(4,128)S(1)} all-to-all(f32[64,4,128]{2,1,0:T(4,128)S(1)} %window_totals.3), channel_id=1, replica_groups=mesh['win'=8,'frame'=64] {'frame'}, dimensions={0} | all-to-all | bytes 262144 | tf_op jit(solution)/shard_map/all_to_all | solution.py:146
  109.9 0.1 reduce_max.9
  110.0 0.1 exponential_reduce_fusion
  110.1 0.6 negate_bitcast_fusion
  (1 shorter events, 0.0 us)
Async XLA Ops:
  0.0 0.7 copy-start.6
  0.7 0.7 copy-start.7
  2.8 34.0 %all-to-all-start = ((f32[64,4,128]{2,1,0:T(4,128)}), f32[64,4,128]{2,1,0:T(4,128)S(1)}, u32[]{:S(2)}, u32[]{:S(2)}) async-start(f32[64,4,128]{2,1,0:T(4,128)} %count_windows.1), calls=%async_computation | async-start | bytes 262144 | tf_op jit(solution)/shard_map/all_to_all | solution.py:146
  21.9 1.0 copy-start.3
  22.9 0.8 copy-start.4
  23.7 0.8 copy-start.5
  24.6 29.0 %copy-start.8 = (s32[64]{0:T(128)S(1)}, s32[64]{0:T(128)}, u32[]{:S(2)}) copy-start(s32[64]{0:T(128)} %lengths_ref.5) | copy-start | bytes 772
  28.6 1.9 %copy-start = (f32[512,2048]{1,0:T(8,128)}, f32[512,2048]{1,0:T(8,128)S(1)}, u32[]{:S(2)}) copy-start(f32[512,2048]{1,0:T(8,128)S(1)} %energies.1.energy_ref) | copy-start | bytes 12582916
  36.8 2.2 %copy-start.1 = (f32[512,2048]{1,0:T(8,128)S(1)}, f32[512,2048]{1,0:T(8,128)}, u32[]{:S(2)}) copy-start(f32[512,2048]{1,0:T(8,128)} %copy-done) | copy-start | bytes 12582916
  39.0 14.6 %copy-start.2 = (f32[512,2048]{1,0:T(8,128)S(1)}, f32[512,2048]{1,0:T(8,128)}, u32[]{:S(2)}) copy-start(f32[512,2048]{1,0:T(8,128)} %copy-done) | copy-start | bytes 12582916

commit v3 on v1

v3 whole, which is shorter than its diff:
```python
import functools
import math

import jax
import jax.numpy as jnp
from jax import lax
from jax.experimental import pallas as pl
from jax.experimental.pallas import tpu as pltpu
from jax.sharding import PartitionSpec as P


ITERS = 2
LANES = 128
ROWS = 64
STEP = 512

floor_value = -1e30
log2_e = 1.0 / math.log(2.0)
least_sum = 2.0**-80
most_sum = 2.0**100

in_vmem = pl.BlockSpec(memory_space=pltpu.VMEM)
in_hbm = pl.BlockSpec(memory_space=pltpu.HBM)
grant = pltpu.CompilerParams(vmem_limit_bytes=12 << 20)
wide_grant = pltpu.CompilerParams(vmem_limit_bytes=52 * 10**6)


def log2(values):
    return jnp.log(values) * log2_e


def log2_sum(values):
    highest = jnp.max(values, axis=0)
    return highest + log2(jnp.sum(jnp.exp2(values - highest[None]), axis=0))


def together(pairs, sems):
    copies = [pltpu.make_async_copy(*pair, sems.at[place]) for place, pair in enumerate(pairs)]
    for copy in copies:
        copy.start()
    for copy in copies:
        copy.wait()


def count_kernel(lengths_hbm, ids_hbm, out_hbm, lengths_ref, ids_ref, out_ref, in_sems, out_sem):
    together([(lengths_hbm, lengths_ref), (ids_hbm, ids_ref)], in_sems)
    groups = out_ref.shape[1]
    capacity = ids_ref.shape[1]
    own_length = lengths_ref[lax.axis_index("frame")]
    local = ids_ref[...] - lax.axis_index("win") * (groups * LANES)
    slots = lax.broadcasted_iota(jnp.int32, (1, capacity), 1)
    local = jnp.where(slots < own_length, local, -1)
    group = jnp.where(local < 0, -1, lax.shift_right_logical(local, 7))
    place = jnp.bitwise_and(local, LANES - 1)
    in_group = lax.broadcasted_iota(jnp.int32, (8, capacity), 0) == group
    in_place = lax.broadcasted_iota(jnp.int32, (LANES, capacity), 0) == place
    counts = lax.dot_general(
        in_group.astype(jnp.float32).astype(jnp.bfloat16),
        in_place.astype(jnp.float32).astype(jnp.bfloat16),
        (((1,), (1,)), ((), ())),
        preferred_element_type=jnp.float32,
    )
    out_ref[...] = jnp.broadcast_to(counts[None, :groups], out_ref.shape)
    copy = pltpu.make_async_copy(out_ref, out_hbm, out_sem)
    copy.start()
    copy.wait()


def energy_kernel(
    lengths_hbm, stiffness_hbm, centers_hbm, distances_hbm, fall_hbm, tops_hbm,
    lengths_ref, stiffness_ref, centers_ref, distances_ref, fall_ref, tops_ref, in_sems, fall_sems, tops_sem,
):
    together(
        [
            (lengths_hbm, lengths_ref),
            (stiffness_hbm, stiffness_ref),
            (centers_hbm, centers_ref),
            (distances_hbm, distances_ref),
        ],
        in_sems,
    )
    own_length = lengths_ref[lax.axis_index("frame")]
    stiffness, centers = stiffness_ref[...] * log2_e, centers_ref[...]
    constant = jnp.sum(-0.5 * stiffness * centers * centers, axis=0, keepdims=True)
    first = lax.broadcasted_iota(jnp.int32, (8, constant.shape[1]), 0) == 0
    constant_rows = jnp.where(first, jnp.broadcast_to(constant, first.shape), 0.0)
    coef_rows = jnp.concatenate([stiffness * centers, -0.5 * stiffness, constant_rows], axis=0).T
    unit_rows = jnp.where(lax.broadcasted_iota(jnp.int32, (8, STEP), 0) == 0, 1.0, 0.0)
    steps = distances_ref.shape[1] // STEP

    def columns(step):
        return pl.ds(pl.multiple_of(step * STEP, STEP), STEP)

    def send(step):
        return pltpu.make_async_copy(
            fall_ref.at[:, columns(step)], fall_hbm.at[:, columns(step)], fall_sems.at[step]
        )

    def one(step, carry):
        separations = distances_ref[:, columns(step)]
        features = jnp.concatenate([separations, separations * separations, unit_rows], axis=0)
        exponents = jnp.dot(
            coef_rows, features, precision=lax.Precision.HIGHEST, preferred_element_type=jnp.float32
        )
        top = jnp.max(exponents, axis=0, keepdims=True)
        fall_ref[:, columns(step)] = exponents - top
        send(step).start()
        for part in range(STEP // LANES):
            tops_ref[0, pl.ds(step * (STEP // LANES) + part, 1), :] = top[:, part * LANES : (part + 1) * LANES]
        return carry

    lax.fori_loop(0, steps, one, 0)
    blocks = tops_ref.shape[1]
    slots = (
        lax.broadcasted_iota(jnp.int32, (blocks, LANES), 0) * LANES
        + lax.broadcasted_iota(jnp.int32, (blocks, LANES), 1)
    )
    tops_ref[1] = jnp.where(slots < own_length, tops_ref[0], floor_value)
    copy = pltpu.make_async_copy(tops_ref, tops_hbm, tops_sem)
    copy.start()
    copy.wait()
    for step in range(steps):
        send(step).wait()


def denominators(shifted, arrive, fall_ref, tops_ref, out_ref, column_ref, part_ref, row_ref):
    groups = shifted.shape[0]
    most = jnp.max(jnp.max(shifted, axis=0, keepdims=True), axis=1, keepdims=True)
    for group in range(groups):
        spread = jnp.broadcast_to(shifted[group : group + 1] - most, (LANES, LANES))
        column_ref[group * LANES : (group + 1) * LANES, :] = spread.T
    windows, capacity = fall_ref.shape
    blocks = capacity // LANES
    chunks = [slice(start, start + ROWS) for start in range(0, windows, ROWS)]

    def columns(block):
        return pl.ds(pl.multiple_of(block * LANES, LANES), LANES)

    def one(block, carry):
        sums = [
            jnp.sum(
                jnp.exp2(fall_ref[rows, columns(block)] + column_ref[rows, :]).reshape(-1, 8, LANES), axis=0
            )
            for rows in chunks
        ]
        part_ref[block] = functools.reduce(jnp.add, sums)
        return carry

    steps = capacity // STEP
    for step in range(steps):
        arrive(step)
        lax.fori_loop(step * (STEP // LANES), (step + 1) * (STEP // LANES), one, 0, unroll=True)
    totals = jnp.sum(part_ref[...], axis=1)
    row_ref[...] = tops_ref[...] + most + log2(totals)

    @pl.when(jnp.min(totals) < least_sum)
    def _():
        def exact(block, carry):
            tops = [
                jnp.max((fall_ref[rows, columns(block)] + column_ref[rows, :]).reshape(-1, 8, LANES), axis=0)
                for rows in chunks
            ]
            highest = jnp.max(functools.reduce(jnp.maximum, tops), axis=0, keepdims=True)
            sums = [
                jnp.sum(
                    jnp.exp2(fall_ref[rows, columns(block)] + column_ref[rows, :] - highest).reshape(-1, 8, LANES),
                    axis=0,
                )
                for rows in chunks
            ]
            total = jnp.sum(functools.reduce(jnp.add, sums), axis=0, keepdims=True)
            row_ref[pl.ds(block, 1), :] = tops_ref[pl.ds(block, 1), :] + most + highest + log2(total)
            return carry

        lax.fori_loop(0, blocks, exact, 0)

    out_ref[...] = jnp.broadcast_to(row_ref[...][None], out_ref.shape)


def first_kernel(
    shared_ref, fall_hbm, tops_hbm, counts_ref, out_ref, fall_ref, tops_ref, column_ref, part_ref, row_ref, sems, tops_sem
):
    def fetch(step):
        columns = slice(step * STEP, (step + 1) * STEP)
        return pltpu.make_async_copy(fall_hbm.at[:, columns], fall_ref.at[:, columns], sems.at[step])

    tops_copy = pltpu.make_async_copy(tops_hbm, tops_ref, tops_sem)
    for step in range(fall_hbm.shape[1] // STEP):
        fetch(step).start()
    tops_copy.start()
    counts = jnp.sum(shared_ref[...], axis=0)
    counts_ref[...] = counts
    shifted = jnp.where(counts > 0.5, log2(jnp.maximum(counts, 1.0)), floor_value)
    tops_copy.wait()
    denominators(
        shifted, lambda step: fetch(step).wait(), fall_ref, tops_ref.at[0], out_ref, column_ref, part_ref, row_ref
    )


def next_kernel(shared_ref, counts_ref, fall_ref, tops_ref, out_ref, column_ref, part_ref, row_ref):
    counts = counts_ref[...]
    free_energy = -log2_sum(shared_ref[...])
    shifted = jnp.where(counts > 0.5, log2(jnp.maximum(counts, 1.0)) + free_energy, floor_value)
    denominators(
        shifted, lambda step: None, fall_ref, tops_ref.at[0], out_ref, column_ref, part_ref, row_ref
    )


def window_kernel(shared_ref, fall_ref, tops_ref, out_ref, den_ref, top_ref, sum_ref, row_ref):
    blocks, windows = shared_ref.shape[1], fall_ref.shape[0]
    groups = windows // LANES
    den_ref[...] = log2_sum(shared_ref[...]) - tops_ref[1]

    def rows_of(chunk):
        return pl.ds(pl.multiple_of(chunk * ROWS, ROWS), ROWS)

    def exponents(rows, block):
        return fall_ref[rows, block * LANES : (block + 1) * LANES] - den_ref[block : block + 1, :]

    def one(chunk, carry):
        rows = rows_of(chunk)
        total = jnp.exp2(exponents(rows, 0))
        for block in range(1, blocks):
            total = total + jnp.exp2(exponents(rows, block))
        sum_ref[rows, :] = total
        return carry

    lax.fori_loop(0, windows // ROWS, one, 0)
    least, most = [], []
    for group in range(groups):
        total = jnp.sum(sum_ref[group * LANES : (group + 1) * LANES, :].T, axis=0, keepdims=True)
        row_ref[group : group + 1, :] = log2(total)
        least.append(total)
        most.append(total)
    lowest = jnp.min(functools.reduce(jnp.minimum, least))
    highest = jnp.max(functools.reduce(jnp.maximum, most))

    @pl.when(jnp.logical_not(jnp.logical_and(lowest > least_sum, highest < most_sum)))
    def _():
        def exact(chunk, carry):
            rows = rows_of(chunk)
            top = exponents(rows, 0)
            for block in range(1, blocks):
                top = jnp.maximum(top, exponents(rows, block))
            total = jnp.exp2(exponents(rows, 0) - top)
            for block in range(1, blocks):
                total = total + jnp.exp2(exponents(rows, block) - top)
            top_ref[rows, :] = top
            sum_ref[rows, :] = total
            return carry

        lax.fori_loop(0, windows // ROWS, exact, 0)
        for group in range(groups):
            rows = slice(group * LANES, (group + 1) * LANES)
            tops, sums = top_ref[rows, :].T, sum_ref[rows, :].T
            top = jnp.max(tops, axis=0, keepdims=True)
            total = jnp.sum(sums * jnp.exp2(tops - top), axis=0, keepdims=True)
            row_ref[group : group + 1, :] = top + log2(total)

    out_ref[...] = jnp.broadcast_to(row_ref[...][None], out_ref.shape)


def exchange(copies, axis):
    return lax.all_to_all(copies, axis, split_axis=0, concat_axis=0, tiled=True)


def on_device(distances, sample_ids, lengths, stiffness, centers):
    windows, capacity = stiffness.shape[0], distances.shape[1]
    groups, blocks, steps = windows // LANES, capacity // LANES, capacity // STEP
    f32, dma = jnp.float32, pltpu.SemaphoreType.DMA
    to_frame = jax.ShapeDtypeStruct((lax.axis_size("frame"), groups, LANES), f32)
    to_win = jax.ShapeDtypeStruct((lax.axis_size("win"), blocks, LANES), f32)
    lengths_here = pltpu.SMEM(lengths.shape, jnp.int32)
    local_counts = pl.pallas_call(
        count_kernel,
        out_shape=to_frame,
        in_specs=[in_hbm] * 2,
        out_specs=in_hbm,
        scratch_shapes=[
            lengths_here,
            pltpu.VMEM((1, capacity), jnp.int32),
            pltpu.VMEM(to_frame.shape, f32),
            dma((2,)),
            dma,
        ],
        name="count_windows",
    )(lengths, sample_ids.reshape(1, capacity))
    shared = exchange(local_counts, "frame")
    energy_shapes = (
        jax.ShapeDtypeStruct((windows, capacity), f32),
        jax.ShapeDtypeStruct((2, blocks, LANES), f32),
    )
    fall, tops = pl.pallas_call(
        energy_kernel,
        out_shape=energy_shapes,
        in_specs=[in_hbm] * 4,
        out_specs=(in_hbm, in_hbm),
        scratch_shapes=[
            lengths_here,
            pltpu.VMEM((stiffness.shape[1], windows), f32),
            pltpu.VMEM((stiffness.shape[1], windows), f32),
            pltpu.VMEM(distances.shape, f32),
            pltpu.VMEM((windows, capacity), f32),
            pltpu.VMEM((2, blocks, LANES), f32),
            dma((4,)),
            dma((steps,)),
            dma,
        ],
        cost_estimate=pl.CostEstimate(
            flops=24 * distances.shape[0] * windows * capacity,
            bytes_accessed=4 * windows * capacity,
            transcendentals=0,
        ),
        name="energies",
    )(lengths, stiffness.T, centers.T, distances)
    den_scratch = [
        pltpu.VMEM((windows, LANES), f32),
        pltpu.VMEM((blocks, 8, LANES), f32),
        pltpu.VMEM((blocks, LANES), f32),
    ]
    counts, own_den, fall, tops = pl.pallas_call(
        first_kernel,
        out_shape=(jax.ShapeDtypeStruct((groups, LANES), f32), to_win, *energy_shapes),
        in_specs=[in_vmem, in_hbm, in_hbm],
        out_specs=(in_vmem,) * 4,
        scratch_shapes=[
            *den_scratch,
            dma((steps,)),
            dma,
        ],
        compiler_params=wide_grant,
        name="first_denominators",
    )(shared, fall, tops)
    for iteration in range(ITERS):
        own_total = pl.pallas_call(
            window_kernel,
            out_shape=to_frame,
            in_specs=[in_vmem] * 3,
            out_specs=in_vmem,
            scratch_shapes=[
                pltpu.VMEM((blocks, LANES), f32),
                pltpu.VMEM((windows, LANES), f32),
                pltpu.VMEM((windows, LANES), f32),
                pltpu.VMEM((groups, LANES), f32),
            ],
            compiler_params=grant,
            name="window_totals",
        )(exchange(own_den, "win"), fall, tops)
        shared = exchange(own_total, "frame")
        if iteration < ITERS - 1:
            own_den = pl.pallas_call(
                next_kernel,
                out_shape=to_win,
                in_specs=[in_vmem] * 4,
                out_specs=in_vmem,
                scratch_shapes=den_scratch,
                compiler_params=grant,
                name="next_denominators",
            )(shared, counts, fall, tops)
    return (-math.log(2.0) * log2_sum(shared)).reshape(windows)


def solution(mesh):
    return jax.shard_map(
        on_device,
        mesh=mesh,
        in_specs=(P(None, "frame"), P("frame"), P(), P("win", None), P("win", None)),
        out_specs=P("win"),
        check_vma=False,
    )
```

time: 123 us -> 108 us (0.88)
  other arithmetic: 18.7 us -> 0.76 us
  Pallas kernels: 0 us -> 16.6 us
  waiting for transfers between devices: 12.9 us -> 8.16 us
  matrix products: 4.68 us -> 0 us
  local copies, waits for them, and re-layouts: 4.8 us -> 0.72 us
    pallas_call x0 -> x6, Pallas kernels: none -> 16.6 us  [the longest x1 6.73 us: on_device(): pl.pallas_call(energy_kernel, out_shape=energy_shapes, in_specs=[in_hbm]...]
    reduce_max x7 -> x1, other arithmetic: 8.81 us -> 0.08 us  [log2_sum(): highest = jnp.max(values, axis=0)]
    reduce_sum x11 -> x1, other arithmetic: 5.14 us -> 0.09 us  [log2_sum(): return highest + log2(jnp.sum(jnp.exp2(values - highest[None]), axis=0))]
    all_to_all x1, waiting for transfers between devices: 12.9 us -> 8.16 us  [exchange(): return lax.all_to_all(copies, axis, split_axis=0, concat_axis=0, tiled=True)]
    dot_general x1 -> x0, matrix products: 4.68 us -> none  [energies(): jnp.dot(coef_rows, features(separations), precision=lax.Precision.HIGHEST...]
    select_n x5 -> x0, other arithmetic: 2.97 us -> none  [the longest x2 1.61 us: on_device(): log_den = jnp.where(slot_usable, log_den, -floor_value)]
    unnamed x8 -> x2, local copies, waits for them, and re-layouts: 2.62 us -> 0.72 us
    dynamic_slice x1 -> x0, local copies, waits for them, and re-layouts: 1.24 us -> none  [on_device(): lax.dynamic_index_in_dim(lengths, lax.axis_index('frame'), keepdims=False)]
  transfers between devices with their start and end apart: 1 -> 1, of which waited for: 1 -> 1; matrix products, arithmetic and copies ran while one was open for 2% -> 0% of each run, Pallas kernels for 0% -> 6%
where the time goes in v3:
time: 108 us; the launch traced here: 107 us
  blocking collectives  61.6 us (57%)
  starting transfers between devices  19.1 us (18%)
  Pallas kernels  16.6 us (15%)
  waiting for transfers between devices  8.16 us (8%)
    all_to_all x4, blocking collectives, exchange(): return lax.all_to_all(copies, axis, split_axis=0, concat_axis=0, tiled=True)  61.6 us
    all_to_all x1, starting transfers between devices, exchange(): return lax.all_to_all(copies, axis, split_axis=0, concat_axis=0, tiled=True)  19.1 us
    all_to_all x1, waiting for transfers between devices, exchange(): return lax.all_to_all(copies, axis, split_axis=0, concat_axis=0, tiled=True)  8.16 us
    pallas_call x1, Pallas kernels, on_device(): pl.pallas_call(energy_kernel, out_shape=energy_shapes, in_specs=[in_hbm]...  6.73 us
    pallas_call x2, Pallas kernels, on_device(): pl.pallas_call(window_kernel, out_shape=to_frame, in_specs=[in_vmem] * 3,...  4.57 us
    pallas_call x1, Pallas kernels, on_device(): pl.pallas_call(first_kernel, out_shape=(jax.ShapeDtypeStruct((groups, LAN...  2.56 us
  transfers between devices with their start and end apart: 1, of which 1 were waited for; matrix products, arithmetic and copies ran while one was open for 0% of the time, Pallas kernels for 6%

profile of v3, /device:TPU:1, one launch (start us, length us, event | category | flops | bytes accessed | tf_op | source)
XLA Modules:
  0.0 107.0 jit_solution(6606955268396459403)
XLA Ops:
  0.0 1.6 %count_windows.1 = f32[64,4,128]{2,1,0:T(4,128)} custom-call(s32[64]{0:T(128)} %lengths_hbm.3, s32[1,2048]{1,0:T(1,128)} %bitcast.5), custom_call_target="tpu_custom_call" | custom-call | tf_op jit(solution)/shard_map/count_windows/pallas_call | solution.py:274
  1.6 19.1 %all-to-all-start = ((f32[64,4,128]{2,1,0:T(4,128)}), f32[64,4,128]{2,1,0:T(4,128)S(1)}, u32[]{:S(2)}, u32[]{:S(2)}) async-start(f32[64,4,128]{2,1,0:T(4,128)} %count_windows.1), calls=%async_computation | async-start | bytes 262144 | tf_op jit(solution)/shard_map/all_to_all | solution.py:264
  20.8 6.7 %energies.1 = (f32[512,2048]{1,0:T(8,128)}, f32[2,16,128]{2,1,0:T(8,128)}) custom-call(s32[64]{0:T(128)} %lengths_hbm.3, f32[32,512]{1,0:T(8,128)} %bitcast.6, f32[32,512]{1,0:T(8,128)} %bitcast.7, f32[32,2048]{1,0:T(8,128)} %distances_hbm.1), custom_call_target="tpu_custom_call" | custom-call | flops 805306368 | bytes 4194304 | tf_op jit(solution)/shard_map/energies/pallas_call | solution.py:293
  27.5 8.2 %all-to-all-done.shared_ref = f32[64,4,128]{2,1,0:T(4,128)S(1)} async-done(((f32[64,4,128]{2,1,0:T(4,128)}), f32[64,4,128]{2,1,0:T(4,128)S(1)}, u32[]{:S(2)}, u32[]{:S(2)}) %all-to-all-start) | async-done | bytes 131104 | tf_op jit(solution)/shard_map/all_to_all | solution.py:264
  35.7 0.0 copy-start
  35.7 0.7 copy-done
  36.4 2.6 %first_denominators.1 = (f32[4,128]{1,0:T(4,128)S(1)}, f32[8,16,128]{2,1,0:T(8,128)S(1)}, f32[512,2048]{1,0:T(8,128)S(1)}, f32[2,16,128]{2,1,0:T(8,128)S(1)}) custom-call(f32[64,4,128]{2,1,0:T(4,128)S(1)} %all-to-all-done.shared_ref, f32[512,2048]{1,0:T(8,128)} %get-tuple-element.11.fall_hbm, f32[2,16,128]{2,1,0:T(8,128)S(1)} %copy-done), custom_call_target="tpu_custom_call" | custom-call | tf_op jit(solution)/shard_map/first_denominators/pallas_call | solution.py:321
  39.0 12.8 %all_to_all.25.shared_ref = f32[8,16,128]{2,1,0:T(8,128)S(1)} all-to-all(f32[8,16,128]{2,1,0:T(8,128)S(1)} %get-tuple-element.13), channel_id=1, replica_groups=mesh['win'=8,'frame'=64] {'win'}, dimensions={0} | all-to-all | bytes 131072 | tf_op jit(solution)/shard_map/all_to_all | solution.py:264
  51.8 2.3 %window_totals.2 = f32[64,4,128]{2,1,0:T(4,128)S(1)} custom-call(f32[8,16,128]{2,1,0:T(8,128)S(1)} %all_to_all.25.shared_ref, f32[512,2048]{1,0:T(8,128)S(1)} %get-tuple-element.14.fall_ref, f32[2,16,128]{2,1,0:T(8,128)S(1)} %get-tuple-element.15.tops_ref), custom_call_target="tpu_custom_call" | custom-call | tf_op jit(solution)/shard_map/window_totals/pallas_call | solution.py:335
  54.1 19.1 %all_to_all.26.shared_ref = f32[64,4,128]{2,1,0:T(4,128)S(1)} all-to-all(f32[64,4,128]{2,1,0:T(4,128)S(1)} %window_totals.2), channel_id=1, replica_groups=mesh['win'=8,'frame'=64] {'frame'}, dimensions={0} | all-to-all | bytes 262144 | tf_op jit(solution)/shard_map/all_to_all | solution.py:264
  73.2 1.1 next_denominators.1
  74.3 10.7 %all_to_all.27.shared_ref = f32[8,16,128]{2,1,0:T(8,128)S(1)} all-to-all(f32[8,16,128]{2,1,0:T(8,128)S(1)} %next_denominators.1), channel_id=1, replica_groups=mesh['win'=8,'frame'=64] {'win'}, dimensions={0} | all-to-all | bytes 131072 | tf_op jit(solution)/shard_map/all_to_all | solution.py:264
  84.9 2.3 %window_totals.3 = f32[64,4,128]{2,1,0:T(4,128)S(1)} custom-call(f32[8,16,128]{2,1,0:T(8,128)S(1)} %all_to_all.27.shared_ref, f32[512,2048]{1,0:T(8,128)S(1)} %get-tuple-element.14.fall_ref, f32[2,16,128]{2,1,0:T(8,128)S(1)} %get-tuple-element.15.tops_ref), custom_call_target="tpu_custom_call" | custom-call | tf_op jit(solution)/shard_map/window_totals/pallas_call | solution.py:335
  87.2 19.1 %all_to_all.28 = f32[64,4,128]{2,1,0:T(4,128)S(1)} all-to-all(f32[64,4,128]{2,1,0:T(4,128)S(1)} %window_totals.3), channel_id=1, replica_groups=mesh['win'=8,'frame'=64] {'frame'}, dimensions={0} | all-to-all | bytes 262144 | tf_op jit(solution)/shard_map/all_to_all | solution.py:264
  106.3 0.1 reduce_max.9
  106.4 0.1 exponential_reduce_fusion
  106.4 0.6 multiply_bitcast_fusion
Async XLA Ops:
  1.6 34.0 %all-to-all-start = ((f32[64,4,128]{2,1,0:T(4,128)}), f32[64,4,128]{2,1,0:T(4,128)S(1)}, u32[]{:S(2)}, u32[]{:S(2)}) async-start(f32[64,4,128]{2,1,0:T(4,128)} %count_windows.1), calls=%async_computation | async-start | bytes 262144 | tf_op jit(solution)/shard_map/all_to_all | solution.py:264
  35.7 0.7 copy-start

commit v4 on v3

v4 whole, which is shorter than its diff:
```python
import functools
import math

import jax
import jax.numpy as jnp
from jax import lax
from jax.experimental import pallas as pl
from jax.experimental.pallas import tpu as pltpu
from jax.sharding import PartitionSpec as P


ITERS = 2
LANES = 128
ROWS = 64
STEP = 512

floor_value = -1e30
log2_e = 1.0 / math.log(2.0)
FAR = 1
least_sum = 2.0**-80
most_sum = 2.0**100

in_vmem = pl.BlockSpec(memory_space=pltpu.VMEM)
in_hbm = pl.BlockSpec(memory_space=pltpu.HBM)
grant = pltpu.CompilerParams(vmem_limit_bytes=12 << 20)


def log2(values):
    return jnp.log(values) * log2_e


def log2_sum(values):
    highest = jnp.max(values, axis=0)
    return highest + log2(jnp.sum(jnp.exp2(values - highest[None]), axis=0))


def together(pairs, sems):
    copies = [pltpu.make_async_copy(*pair, sems.at[place]) for place, pair in enumerate(pairs)]
    for copy in copies:
        copy.start()
    for copy in copies:
        copy.wait()


def count_kernel(lengths_hbm, ids_hbm, out_hbm, lengths_ref, ids_ref, out_ref, in_sems, out_sem):
    together([(lengths_hbm, lengths_ref), (ids_hbm, ids_ref)], in_sems)
    groups = out_ref.shape[1]
    capacity = ids_ref.shape[1]
    own_length = lengths_ref[lax.axis_index("frame")]
    local = ids_ref[...] - lax.axis_index("win") * (groups * LANES)
    slots = lax.broadcasted_iota(jnp.int32, (1, capacity), 1)
    local = jnp.where(slots < own_length, local, -1)
    group = jnp.where(local < 0, -1, lax.shift_right_logical(local, 7))
    place = jnp.bitwise_and(local, LANES - 1)
    in_group = lax.broadcasted_iota(jnp.int32, (8, capacity), 0) == group
    in_place = lax.broadcasted_iota(jnp.int32, (LANES, capacity), 0) == place
    counts = lax.dot_general(
        in_group.astype(jnp.float32).astype(jnp.bfloat16),
        in_place.astype(jnp.float32).astype(jnp.bfloat16),
        (((1,), (1,)), ((), ())),
        preferred_element_type=jnp.float32,
    )
    out_ref[...] = jnp.broadcast_to(counts[None, :groups], out_ref.shape)
    copy = pltpu.make_async_copy(out_ref, out_hbm, out_sem)
    copy.start()
    copy.wait()


def energy_kernel(
    stiffness_hbm, centers_hbm, distances_hbm, near_ref, tops_ref, far_hbm,
    stiffness_ref, centers_ref, distances_ref, far_ref, in_sems, far_sem,
):
    together(
        [
            (stiffness_hbm, stiffness_ref),
            (centers_hbm, centers_ref),
            (distances_hbm, distances_ref),
        ],
        in_sems,
    )
    stiffness, centers = stiffness_ref[...] * log2_e, centers_ref[...]
    constant = jnp.sum(-0.5 * stiffness * centers * centers, axis=0, keepdims=True)
    first = lax.broadcasted_iota(jnp.int32, (8, constant.shape[1]), 0) == 0
    constant_rows = jnp.where(first, jnp.broadcast_to(constant, first.shape), 0.0)
    coef_rows = jnp.concatenate([stiffness * centers, -0.5 * stiffness, constant_rows], axis=0).T
    unit_rows = jnp.where(lax.broadcasted_iota(jnp.int32, (8, STEP), 0) == 0, 1.0, 0.0)

    def one(step, to_ref, to):
        start = pl.multiple_of(step * STEP, STEP)
        separations = distances_ref[:, pl.ds(start, STEP)]
        features = jnp.concatenate([separations, separations * separations, unit_rows], axis=0)
        exponents = jnp.dot(
            coef_rows, features, precision=lax.Precision.HIGHEST, preferred_element_type=jnp.float32
        )
        top = jnp.max(exponents, axis=0, keepdims=True)
        to_ref[:, pl.ds(to, STEP)] = exponents - top
        for part in range(STEP // LANES):
            tops_ref[pl.ds(step * (STEP // LANES) + part, 1), :] = top[:, part * LANES : (part + 1) * LANES]

    near_steps = near_ref.shape[1] // STEP
    copy = pltpu.make_async_copy(far_ref, far_hbm, far_sem)
    one(near_steps, far_ref, 0)
    copy.start()

    def near(step, carry):
        one(step, near_ref, pl.multiple_of(step * STEP, STEP))
        return carry

    lax.fori_loop(0, near_steps, near, 0)
    copy.wait()


def denominators(shifted, arrive, parts, tops_ref, out_ref, column_ref, part_ref, row_ref):
    groups = shifted.shape[0]
    most = jnp.max(jnp.max(shifted, axis=0, keepdims=True), axis=1, keepdims=True)
    for group in range(groups):
        spread = jnp.broadcast_to(shifted[group : group + 1] - most, (LANES, LANES))
        column_ref[group * LANES : (group + 1) * LANES, :] = spread.T
    windows = column_ref.shape[0]
    chunks = [slice(start, start + ROWS) for start in range(0, windows, ROWS)]

    def exponents(ref, rows, block):
        return (ref[rows, pl.ds(pl.multiple_of(block * LANES, LANES), LANES)] + column_ref[rows, :]).reshape(
            -1, 8, LANES
        )

    done = 0
    for part, ref in enumerate(parts):
        if part:
            arrive()
        count = ref.shape[1] // LANES

        def one(block, carry, ref=ref, done=done):
            sums = [jnp.sum(jnp.exp2(exponents(ref, rows, block)), axis=0) for rows in chunks]
            part_ref[done + block] = functools.reduce(jnp.add, sums)
            return carry

        lax.fori_loop(0, count, one, 0, unroll=4)
        done += count
    totals = jnp.sum(part_ref[...], axis=1)
    out_ref[...] = jnp.broadcast_to((tops_ref[...] + most + log2(totals))[None], out_ref.shape)

    @pl.when(jnp.min(totals) < least_sum)
    def _():
        done = 0
        for ref in parts:
            count = ref.shape[1] // LANES

            def exact(block, carry, ref=ref, done=done):
                tops = [jnp.max(exponents(ref, rows, block), axis=0) for rows in chunks]
                highest = jnp.max(functools.reduce(jnp.maximum, tops), axis=0, keepdims=True)
                sums = [jnp.sum(jnp.exp2(exponents(ref, rows, block) - highest), axis=0) for rows in chunks]
                total = jnp.sum(functools.reduce(jnp.add, sums), axis=0, keepdims=True)
                row_ref[pl.ds(done + block, 1), :] = highest + log2(total)
                return carry

            lax.fori_loop(0, count, exact, 0)
            done += count
        out_ref[...] = jnp.broadcast_to((tops_ref[...] + most + row_ref[...])[None], out_ref.shape)


def first_kernel(
    lengths_hbm, shared_ref, near_ref, tops_ref, far_hbm, counts_ref, out_ref, far_ref, used_ref,
    column_ref, part_ref, row_ref, lengths_ref, sem, lengths_sem,
):
    copy = pltpu.make_async_copy(far_hbm, far_ref, sem)
    lengths_copy = pltpu.make_async_copy(lengths_hbm, lengths_ref, lengths_sem)
    copy.start()
    lengths_copy.start()
    counts = jnp.sum(shared_ref[...], axis=0)
    counts_ref[...] = counts
    shifted = jnp.where(counts > 0.5, log2(jnp.maximum(counts, 1.0)), floor_value)
    denominators(shifted, copy.wait, (near_ref, far_ref), tops_ref, out_ref, column_ref, part_ref, row_ref)
    lengths_copy.wait()
    own_length = lengths_ref[lax.axis_index("frame")]
    slots = (
        lax.broadcasted_iota(jnp.int32, tops_ref.shape, 0) * LANES
        + lax.broadcasted_iota(jnp.int32, tops_ref.shape, 1)
    )
    used_ref[...] = jnp.where(slots < own_length, tops_ref[...], floor_value)


def next_kernel(shared_ref, counts_ref, near_ref, tops_ref, far_ref, out_ref, column_ref, part_ref, row_ref):
    counts = counts_ref[...]
    free_energy = -log2_sum(shared_ref[...])
    shifted = jnp.where(counts > 0.5, log2(jnp.maximum(counts, 1.0)) + free_energy, floor_value)
    denominators(shifted, lambda: None, (near_ref, far_ref), tops_ref, out_ref, column_ref, part_ref, row_ref)


def window_kernel(shared_ref, near_ref, used_ref, far_ref, out_ref, den_ref, top_ref, sum_ref, row_ref):
    windows, near_blocks, far_blocks = near_ref.shape[0], near_ref.shape[1] // LANES, far_ref.shape[1] // LANES
    groups = windows // LANES
    den_ref[...] = log2_sum(shared_ref[...]) - used_ref[...]

    def exponents(chunk):
        rows = pl.ds(pl.multiple_of(chunk * ROWS, ROWS), ROWS)
        for ref, done in ((near_ref, 0), (far_ref, near_blocks)):
            for block in range(ref.shape[1] // LANES):
                yield ref[rows, block * LANES : (block + 1) * LANES] - den_ref[done + block : done + block + 1, :]

    def one(chunk, carry):
        rows = pl.ds(pl.multiple_of(chunk * ROWS, ROWS), ROWS)
        sum_ref[rows, :] = functools.reduce(jnp.add, (jnp.exp2(each) for each in exponents(chunk)))
        return carry

    lax.fori_loop(0, windows // ROWS, one, 0)
    totals = []
    for group in range(groups):
        total = jnp.sum(sum_ref[group * LANES : (group + 1) * LANES, :].T, axis=0, keepdims=True)
        totals.append(total)
        row_ref[group : group + 1, :] = log2(total)
    out_ref[...] = jnp.broadcast_to(row_ref[...][None], out_ref.shape)
    lowest = jnp.min(functools.reduce(jnp.minimum, totals))
    highest = jnp.max(functools.reduce(jnp.maximum, totals))

    @pl.when(jnp.logical_not(jnp.logical_and(lowest > least_sum, highest < most_sum)))
    def _():
        def exact(chunk, carry):
            rows = pl.ds(pl.multiple_of(chunk * ROWS, ROWS), ROWS)
            top = functools.reduce(jnp.maximum, exponents(chunk))
            top_ref[rows, :] = top
            sum_ref[rows, :] = functools.reduce(jnp.add, (jnp.exp2(each - top) for each in exponents(chunk)))
            return carry

        lax.fori_loop(0, windows // ROWS, exact, 0)
        for group in range(groups):
            rows = slice(group * LANES, (group + 1) * LANES)
            tops, sums = top_ref[rows, :].T, sum_ref[rows, :].T
            top = jnp.max(tops, axis=0, keepdims=True)
            total = jnp.sum(sums * jnp.exp2(tops - top), axis=0, keepdims=True)
            row_ref[group : group + 1, :] = top + log2(total)
        out_ref[...] = jnp.broadcast_to(row_ref[...][None], out_ref.shape)


def exchange(copies, axis):
    return lax.all_to_all(copies, axis, split_axis=0, concat_axis=0, tiled=True)


def on_device(distances, sample_ids, lengths, stiffness, centers):
    windows, capacity = stiffness.shape[0], distances.shape[1]
    groups, blocks, steps = windows // LANES, capacity // LANES, capacity // STEP
    f32, dma = jnp.float32, pltpu.SemaphoreType.DMA
    to_frame = jax.ShapeDtypeStruct((lax.axis_size("frame"), groups, LANES), f32)
    to_win = jax.ShapeDtypeStruct((lax.axis_size("win"), blocks, LANES), f32)
    lengths_here = pltpu.SMEM(lengths.shape, jnp.int32)
    local_counts = pl.pallas_call(
        count_kernel,
        out_shape=to_frame,
        in_specs=[in_hbm] * 2,
        out_specs=in_hbm,
        scratch_shapes=[
            lengths_here,
            pltpu.VMEM((1, capacity), jnp.int32),
            pltpu.VMEM(to_frame.shape, f32),
            dma((2,)),
            dma,
        ],
        name="count_windows",
    )(lengths, sample_ids.reshape(1, capacity))
    shared = exchange(local_counts, "frame")
    far_frames = FAR * STEP
    near_shape = jax.ShapeDtypeStruct((windows, capacity - far_frames), f32)
    far_shape = jax.ShapeDtypeStruct((windows, far_frames), f32)
    tops_shape = jax.ShapeDtypeStruct((blocks, LANES), f32)
    near, tops, far = pl.pallas_call(
        energy_kernel,
        out_shape=(near_shape, tops_shape, far_shape),
        in_specs=[in_hbm] * 3,
        out_specs=(in_vmem, in_vmem, in_hbm),
        scratch_shapes=[
            pltpu.VMEM((stiffness.shape[1], windows), f32),
            pltpu.VMEM((stiffness.shape[1], windows), f32),
            pltpu.VMEM(distances.shape, f32),
            pltpu.VMEM(far_shape.shape, f32),
            dma((3,)),
            dma,
        ],
        compiler_params=grant,
        cost_estimate=pl.CostEstimate(
            flops=24 * distances.shape[0] * windows * capacity,
            bytes_accessed=4 * windows * capacity,
            transcendentals=0,
        ),
        name="energies",
    )(stiffness.T, centers.T, distances)
    den_scratch = [
        pltpu.VMEM((windows, LANES), f32),
        pltpu.VMEM((blocks, 8, LANES), f32),
        pltpu.VMEM((blocks, LANES), f32),
    ]
    counts, own_den, far, used = pl.pallas_call(
        first_kernel,
        out_shape=(jax.ShapeDtypeStruct((groups, LANES), f32), to_win, far_shape, tops_shape),
        in_specs=[in_hbm, in_vmem, in_vmem, in_vmem, in_hbm],
        out_specs=(in_vmem,) * 4,
        scratch_shapes=[*den_scratch, lengths_here, dma, dma],
        compiler_params=grant,
        name="first_denominators",
    )(lengths, shared, near, tops, far)
    for iteration in range(ITERS):
        own_total = pl.pallas_call(
            window_kernel,
            out_shape=to_frame,
            in_specs=[in_vmem] * 4,
            out_specs=in_vmem,
            scratch_shapes=[
                pltpu.VMEM((blocks, LANES), f32),
                pltpu.VMEM((windows, LANES), f32),
                pltpu.VMEM((windows, LANES), f32),
                pltpu.VMEM((groups, LANES), f32),
            ],
            compiler_params=grant,
            name="window_totals",
        )(exchange(own_den, "win"), near, used, far)
        shared = exchange(own_total, "frame")
        if iteration < ITERS - 1:
            own_den = pl.pallas_call(
                next_kernel,
                out_shape=to_win,
                in_specs=[in_vmem] * 5,
                out_specs=in_vmem,
                scratch_shapes=den_scratch,
                compiler_params=grant,
                name="next_denominators",
            )(shared, counts, near, tops, far)
    return (-math.log(2.0) * log2_sum(shared)).reshape(windows)


def solution(mesh):
    return jax.shard_map(
        on_device,
        mesh=mesh,
        in_specs=(P(None, "frame"), P("frame"), P(), P("win", None), P("win", None)),
        out_specs=P("win"),
        check_vma=False,
    )
```

time: 108 us -> 110 us (1.019)
  local copies, waits for them, and re-layouts: 0.72 us -> 4.81 us
  Pallas kernels: 16.6 us -> 14 us
  waiting for transfers between devices: 8.16 us -> 6.51 us
  blocking collectives: 61.6 us -> 63.1 us
    unnamed x2 -> x12, local copies, waits for them, and re-layouts: 0.72 us -> 4.81 us
    all_to_all x1, waiting for transfers between devices: 8.16 us -> 6.51 us  [exchange(): return lax.all_to_all(copies, axis, split_axis=0, concat_axis=0, tiled=True)]
    pallas_call x4, Pallas kernels: 12.4 us -> 10.8 us  [the longest x1 4.79 us: on_device(): pl.pallas_call(energy_kernel, out_shape=(near_shape, tops_shape, far_shap...]
    all_to_all x4, blocking collectives: 61.6 us -> 63.1 us  [exchange(): return lax.all_to_all(copies, axis, split_axis=0, concat_axis=0, tiled=True)]
    pallas_call x1, Pallas kernels: 2.56 us -> 1.39 us  [on_device(): pl.pallas_call(first_kernel, out_shape=(jax.ShapeDtypeStruct((groups, LAN...]
  transfers between devices with their start and end apart: 1 -> 1, of which waited for: 1 -> 1; matrix products, arithmetic and copies ran while one was open for 0% -> 0% of each run, Pallas kernels for 6% -> 4%
where the time goes in v4:
time: 110 us; the launch traced here: 108 us
  blocking collectives  63.1 us (57%)
  starting transfers between devices  19.1 us (17%)
  Pallas kernels  14 us (13%)
  waiting for transfers between devices  6.51 us (6%)
  local copies, waits for them, and re-layouts  4.81 us (4%)
    all_to_all x4, blocking collectives, exchange(): return lax.all_to_all(copies, axis, split_axis=0, concat_axis=0, tiled=True)  63.1 us
    all_to_all x1, starting transfers between devices, exchange(): return lax.all_to_all(copies, axis, split_axis=0, concat_axis=0, tiled=True)  19.1 us
    all_to_all x1, waiting for transfers between devices, exchange(): return lax.all_to_all(copies, axis, split_axis=0, concat_axis=0, tiled=True)  6.51 us
    unnamed x12, local copies, waits for them, and re-layouts  4.81 us
    pallas_call x1, Pallas kernels, on_device(): pl.pallas_call(energy_kernel, out_shape=(near_shape, tops_shape, far_shap...  4.79 us
    pallas_call x2, Pallas kernels, on_device(): pl.pallas_call(window_kernel, out_shape=to_frame, in_specs=[in_vmem] * 4,...  4.76 us
  transfers between devices with their start and end apart: 1, of which 1 were waited for; matrix products, arithmetic and copies ran while one was open for 0% of the time, Pallas kernels for 4%

profile of v4, /device:TPU:1, one launch (start us, length us, event | category | flops | bytes accessed | tf_op | source)
XLA Modules:
  0.0 108.4 jit_solution(2548124130071998608)
XLA Ops:
  0.0 0.0 copy-start.2
  0.0 1.7 %count_windows.1 = f32[64,4,128]{2,1,0:T(4,128)} custom-call(s32[64]{0:T(128)} %lengths_hbm.3, s32[1,2048]{1,0:T(1,128)} %bitcast.7), custom_call_target="tpu_custom_call" | custom-call | tf_op jit(solution)/shard_map/count_windows/pallas_call | solution.py:246
  1.8 19.1 %all-to-all-start = ((f32[64,4,128]{2,1,0:T(4,128)}), f32[64,4,128]{2,1,0:T(4,128)S(1)}, u32[]{:S(2)}, u32[]{:S(2)}) async-start(f32[64,4,128]{2,1,0:T(4,128)} %count_windows.1), calls=%async_computation | async-start | bytes 262144 | tf_op jit(solution)/shard_map/all_to_all | solution.py:236
  20.9 0.0 copy-start.3
  20.9 0.9 copy-done.3
  21.8 0.0 copy-start.4
  21.8 0.8 copy-done.4
  22.7 0.0 copy-start.5
  22.7 0.8 copy-done.5
  23.5 4.8 %energies.1 = (f32[512,1536]{1,0:T(8,128)S(1)}, f32[16,128]{1,0:T(8,128)S(1)}, f32[512,512]{1,0:T(8,128)S(1)}) custom-call(f32[32,512]{1,0:T(8,128)S(1)} %bitcast.5, f32[32,512]{1,0:T(8,128)S(1)} %bitcast.6, f32[32,2048]{1,0:T(8,128)S(1)} %copy-done.3), custom_call_target="tpu_custom_call" | custom-call | flops 805306368 | bytes 4194304 | tf_op jit(solution)/shard_map/energies/pallas_call | solution.py:265
  28.3 0.0 copy-start
  28.3 1.0 copy-done
  29.3 6.5 %all-to-all-done.shared_ref = f32[64,4,128]{2,1,0:T(4,128)S(1)} async-done(((f32[64,4,128]{2,1,0:T(4,128)}), f32[64,4,128]{2,1,0:T(4,128)S(1)}, u32[]{:S(2)}, u32[]{:S(2)}) %all-to-all-start) | async-done | bytes 131104 | tf_op jit(solution)/shard_map/all_to_all | solution.py:236
  35.8 0.0 copy-done.2
  35.8 0.0 copy-start.1
  35.8 1.2 %copy-done.1 = f32[512,512]{1,0:T(8,128)S(1)} copy-done((f32[512,512]{1,0:T(8,128)S(1)}, f32[512,512]{1,0:T(8,128)}, u32[]{:S(2)}) %copy-start.1) | copy-done | bytes 1048600
  37.0 1.4 %first_denominators.1 = (f32[4,128]{1,0:T(4,128)S(1)}, f32[8,16,128]{2,1,0:T(8,128)S(1)}, f32[512,512]{1,0:T(8,128)S(1)}, f32[16,128]{1,0:T(8,128)S(1)}) custom-call(s32[64]{0:T(128)S(1)} %copy-done.2, f32[64,4,128]{2,1,0:T(4,128)S(1)} %all-to-all-done.shared_ref, f32[512,1536]{1,0:T(8,128)S(1)} %get-tuple-element.12.near_ref, ...), custom_call_target="tpu_custom_call" | custom-call | tf_op jit(solution)/shard_map/first_denominators/pallas_call | solution.py:291
  38.4 12.8 %all_to_all.25.shared_ref = f32[8,16,128]{2,1,0:T(8,128)S(1)} all-to-all(f32[8,16,128]{2,1,0:T(8,128)S(1)} %get-tuple-element.15), channel_id=1, replica_groups=mesh['win'=8,'frame'=64] {'win'}, dimensions={0} | all-to-all | bytes 131072 | tf_op jit(solution)/shard_map/all_to_all | solution.py:236
  51.3 2.4 %window_totals.2 = f32[64,4,128]{2,1,0:T(4,128)S(1)} custom-call(f32[8,16,128]{2,1,0:T(8,128)S(1)} %all_to_all.25.shared_ref, f32[512,1536]{1,0:T(8,128)S(1)} %get-tuple-element.12.near_ref, f32[16,128]{1,0:T(8,128)S(1)} %get-tuple-element.16.used_ref, f32[512,512]{1,0:T(8,128)S(1)} %get-tuple-element.17.far_ref), custom_call_target="tpu_custom_call" | custom-call | tf_op jit(solution)/shard_map/window_totals/pallas_call | solution.py:301
  53.7 20.3 %all_to_all.26.shared_ref = f32[64,4,128]{2,1,0:T(4,128)S(1)} all-to-all(f32[64,4,128]{2,1,0:T(4,128)S(1)} %window_totals.2), channel_id=1, replica_groups=mesh['win'=8,'frame'=64] {'frame'}, dimensions={0} | all-to-all | bytes 262144 | tf_op jit(solution)/shard_map/all_to_all | solution.py:236
  74.0 1.3 %next_denominators.1 = f32[8,16,128]{2,1,0:T(8,128)S(1)} custom-call(f32[64,4,128]{2,1,0:T(4,128)S(1)} %all_to_all.26.shared_ref, f32[4,128]{1,0:T(4,128)S(1)} %get-tuple-element.18.counts_ref, f32[512,1536]{1,0:T(8,128)S(1)} %get-tuple-element.12.near_ref, f32[16,128]{1,0:T(8,128)S(1)} %get-tuple-element.13.tops_ref, f32[512,512]{1,0:T(8,128)S(1)} %get-tuple-element.17.far_ref), custom_call_target="tpu_custom_call" | custom-call | tf_op jit(solution)/shard_map/next_denominators/pallas_call | solution.py:317
  75.3 10.8 %all_to_all.27.shared_ref = f32[8,16,128]{2,1,0:T(8,128)S(1)} all-to-all(f32[8,16,128]{2,1,0:T(8,128)S(1)} %next_denominators.1), channel_id=1, replica_groups=mesh['win'=8,'frame'=64] {'win'}, dimensions={0} | all-to-all | bytes 131072 | tf_op jit(solution)/shard_map/all_to_all | solution.py:236
  86.1 2.4 %window_totals.3 = f32[64,4,128]{2,1,0:T(4,128)S(1)} custom-call(f32[8,16,128]{2,1,0:T(8,128)S(1)} %all_to_all.27.shared_ref, f32[512,1536]{1,0:T(8,128)S(1)} %get-tuple-element.12.near_ref, f32[16,128]{1,0:T(8,128)S(1)} %get-tuple-element.16.used_ref, f32[512,512]{1,0:T(8,128)S(1)} %get-tuple-element.17.far_ref), custom_call_target="tpu_custom_call" | custom-call | tf_op jit(solution)/shard_map/window_totals/pallas_call | solution.py:301
  88.5 19.1 %all_to_all.28 = f32[64,4,128]{2,1,0:T(4,128)S(1)} all-to-all(f32[64,4,128]{2,1,0:T(4,128)S(1)} %window_totals.3), channel_id=1, replica_groups=mesh['win'=8,'frame'=64] {'frame'}, dimensions={0} | all-to-all | bytes 262144 | tf_op jit(solution)/shard_map/all_to_all | solution.py:236
  107.6 0.1 reduce_max.9
  107.7 0.1 exponential_reduce_fusion
  107.8 0.6 multiply_bitcast_fusion
Async XLA Ops:
  0.0 35.8 %copy-start.2 = (s32[64]{0:T(128)S(1)}, s32[64]{0:T(128)}, u32[]{:S(2)}) copy-start(s32[64]{0:T(128)} %lengths_hbm.3) | copy-start | bytes 772
  1.8 34.0 %all-to-all-start = ((f32[64,4,128]{2,1,0:T(4,128)}), f32[64,4,128]{2,1,0:T(4,128)S(1)}, u32[]{:S(2)}, u32[]{:S(2)}) async-start(f32[64,4,128]{2,1,0:T(4,128)} %count_windows.1), calls=%async_computation | async-start | bytes 262144 | tf_op jit(solution)/shard_map/all_to_all | solution.py:236
  20.9 1.0 copy-start.3
  21.8 0.8 copy-start.4
  22.7 0.8 copy-start.5
  28.3 1.0 copy-start
  35.8 1.2 %copy-start.1 = (f32[512,512]{1,0:T(8,128)S(1)}, f32[512,512]{1,0:T(8,128)}, u32[]{:S(2)}) copy-start(f32[512,512]{1,0:T(8,128)} %copy-done) | copy-start | bytes 3145732

commit v5 on v4

--- a/solution.py
+++ b/solution.py
@@ -23,6 +23,10 @@
 in_vmem = pl.BlockSpec(memory_space=pltpu.VMEM)
 in_hbm = pl.BlockSpec(memory_space=pltpu.HBM)
 grant = pltpu.CompilerParams(vmem_limit_bytes=12 << 20)
+
+
+def hbm(array):
+    return pltpu.with_memory_space_constraint(array, pltpu.HBM)
 
 
 def log2(values):
@@ -135,7 +139,7 @@
             part_ref[done + block] = functools.reduce(jnp.add, sums)
             return carry
 
-        lax.fori_loop(0, count, one, 0, unroll=4)
+        lax.fori_loop(0, count, one, 0, unroll=True)
         done += count
     totals = jnp.sum(part_ref[...], axis=1)
     out_ref[...] = jnp.broadcast_to((tops_ref[...] + most + log2(totals))[None], out_ref.shape)
@@ -264,7 +268,7 @@
     tops_shape = jax.ShapeDtypeStruct((blocks, LANES), f32)
     near, tops, far = pl.pallas_call(
         energy_kernel,
-        out_shape=(near_shape, tops_shape, far_shape),
+        out_shape=(near_shape, tops_shape, pltpu.HBM(far_shape.shape, f32)),
         in_specs=[in_hbm] * 3,
         out_specs=(in_vmem, in_vmem, in_hbm),
         scratch_shapes=[
@@ -282,7 +286,7 @@
             transcendentals=0,
         ),
         name="energies",
-    )(stiffness.T, centers.T, distances)
+    )(hbm(stiffness.T), hbm(centers.T), hbm(distances))
     den_scratch = [
         pltpu.VMEM((windows, LANES), f32),
         pltpu.VMEM((blocks, 8, LANES), f32),
@@ -296,7 +300,7 @@
         scratch_shapes=[*den_scratch, lengths_here, dma, dma],
         compiler_params=grant,
         name="first_denominators",
-    )(lengths, shared, near, tops, far)
+    )(hbm(lengths), shared, near, tops, hbm(far))
     for iteration in range(ITERS):
         own_total = pl.pallas_call(
             window_kernel,

time: 110 us -> 107 us (0.973)
  local copies, waits for them, and re-layouts: 4.81 us -> 0 us
  waiting for transfers between devices: 6.51 us -> 9.37 us
  blocking collectives: 63.1 us -> 61.6 us
    unnamed x12 -> x0, local copies, waits for them, and re-layouts: 4.81 us -> none
    all_to_all x1, waiting for transfers between devices: 6.51 us -> 9.37 us  [exchange(): return lax.all_to_all(copies, axis, split_axis=0, concat_axis=0, tiled=True)]
    all_to_all x4, blocking collectives: 63.1 us -> 61.6 us  [exchange(): return lax.all_to_all(copies, axis, split_axis=0, concat_axis=0, tiled=True)]
  transfers between devices with their start and end apart: 1 -> 1, of which waited for: 1 -> 1; matrix products, arithmetic and copies ran while one was open for 0% -> 0% of each run, Pallas kernels for 4% -> 5%
where the time goes in v5:
time: 107 us; the launch traced here: 105 us
  blocking collectives  61.6 us (58%)
  starting transfers between devices  19.1 us (18%)
  Pallas kernels  14.3 us (13%)
  waiting for transfers between devices  9.37 us (9%)
    all_to_all x4, blocking collectives, exchange(): return lax.all_to_all(copies, axis, split_axis=0, concat_axis=0, tiled=True)  61.6 us
    all_to_all x1, starting transfers between devices, exchange(): return lax.all_to_all(copies, axis, split_axis=0, concat_axis=0, tiled=True)  19.1 us
    all_to_all x1, waiting for transfers between devices, exchange(): return lax.all_to_all(copies, axis, split_axis=0, concat_axis=0, tiled=True)  9.37 us
    pallas_call x1, Pallas kernels, on_device(): pl.pallas_call(energy_kernel, out_shape=(near_shape, tops_shape, pltpu.HB...  5.53 us
    pallas_call x2, Pallas kernels, on_device(): pl.pallas_call(window_kernel, out_shape=to_frame, in_specs=[in_vmem] * 4,...  4.44 us
  transfers between devices with their start and end apart: 1, of which 1 were waited for; matrix products, arithmetic and copies ran while one was open for 0% of the time, Pallas kernels for 5%

profile of v5, /device:TPU:1, one launch (start us, length us, event | category | flops | bytes accessed | tf_op | source)
XLA Modules:
  0.0 105.2 jit_solution(9141065205072255713)
XLA Ops:
  0.0 1.6 %count_windows.1 = f32[64,4,128]{2,1,0:T(4,128)} custom-call(s32[64]{0:T(128)} %lengths_hbm.3, s32[1,2048]{1,0:T(1,128)} %bitcast.5), custom_call_target="tpu_custom_call" | custom-call | tf_op jit(solution)/shard_map/count_windows/pallas_call | solution.py:250
  1.7 19.1 %all-to-all-start = ((f32[64,4,128]{2,1,0:T(4,128)}), f32[64,4,128]{2,1,0:T(4,128)S(1)}, u32[]{:S(2)}, u32[]{:S(2)}) async-start(f32[64,4,128]{2,1,0:T(4,128)} %count_windows.1), calls=%async_computation | async-start | bytes 262144 | tf_op jit(solution)/shard_map/all_to_all | solution.py:240
  20.8 5.5 %energies.1 = (f32[512,1536]{1,0:T(8,128)S(1)}, f32[16,128]{1,0:T(8,128)S(1)}, f32[512,512]{1,0:T(8,128)}) custom-call(f32[32,512]{1,0:T(8,128)} %bitcast.6, f32[32,512]{1,0:T(8,128)} %bitcast.7, f32[32,2048]{1,0:T(8,128)} %distances_hbm.1), custom_call_target="tpu_custom_call" | custom-call | flops 805306368 | bytes 4194304 | tf_op jit(solution)/shard_map/energies/pallas_call | solution.py:269
  26.3 9.4 %all-to-all-done.shared_ref = f32[64,4,128]{2,1,0:T(4,128)S(1)} async-done(((f32[64,4,128]{2,1,0:T(4,128)}), f32[64,4,128]{2,1,0:T(4,128)S(1)}, u32[]{:S(2)}, u32[]{:S(2)}) %all-to-all-start) | async-done | bytes 131104 | tf_op jit(solution)/shard_map/all_to_all | solution.py:240
  35.7 1.6 %first_denominators.1 = (f32[4,128]{1,0:T(4,128)S(1)}, f32[8,16,128]{2,1,0:T(8,128)S(1)}, f32[512,512]{1,0:T(8,128)S(1)}, f32[16,128]{1,0:T(8,128)S(1)}) custom-call(s32[64]{0:T(128)} %lengths_hbm.3, f32[64,4,128]{2,1,0:T(4,128)S(1)} %all-to-all-done.shared_ref, f32[512,1536]{1,0:T(8,128)S(1)} %get-tuple-element.12.near_ref, ...), custom_call_target="tpu_custom_call" | custom-call | tf_op jit(solution)/shard_map/first_denominators/pallas_call | solution.py:295
  37.3 12.8 %all_to_all.25.shared_ref = f32[8,16,128]{2,1,0:T(8,128)S(1)} all-to-all(f32[8,16,128]{2,1,0:T(8,128)S(1)} %get-tuple-element.15), channel_id=1, replica_groups=mesh['win'=8,'frame'=64] {'win'}, dimensions={0} | all-to-all | bytes 131072 | tf_op jit(solution)/shard_map/all_to_all | solution.py:240
  50.1 2.2 %window_totals.2 = f32[64,4,128]{2,1,0:T(4,128)S(1)} custom-call(f32[8,16,128]{2,1,0:T(8,128)S(1)} %all_to_all.25.shared_ref, f32[512,1536]{1,0:T(8,128)S(1)} %get-tuple-element.12.near_ref, f32[16,128]{1,0:T(8,128)S(1)} %get-tuple-element.16.used_ref, f32[512,512]{1,0:T(8,128)S(1)} %get-tuple-element.17.far_ref), custom_call_target="tpu_custom_call" | custom-call | tf_op jit(solution)/shard_map/window_totals/pallas_call | solution.py:305
  52.4 19.1 %all_to_all.26.shared_ref = f32[64,4,128]{2,1,0:T(4,128)S(1)} all-to-all(f32[64,4,128]{2,1,0:T(4,128)S(1)} %window_totals.2), channel_id=1, replica_groups=mesh['win'=8,'frame'=64] {'frame'}, dimensions={0} | all-to-all | bytes 262144 | tf_op jit(solution)/shard_map/all_to_all | solution.py:240
  71.5 1.1 %next_denominators.1 = f32[8,16,128]{2,1,0:T(8,128)S(1)} custom-call(f32[64,4,128]{2,1,0:T(4,128)S(1)} %all_to_all.26.shared_ref, f32[4,128]{1,0:T(4,128)S(1)} %get-tuple-element.18.counts_ref, f32[512,1536]{1,0:T(8,128)S(1)} %get-tuple-element.12.near_ref, f32[16,128]{1,0:T(8,128)S(1)} %get-tuple-element.13.tops_ref, f32[512,512]{1,0:T(8,128)S(1)} %get-tuple-element.17.far_ref), custom_call_target="tpu_custom_call" | custom-call | tf_op jit(solution)/shard_map/next_denominators/pallas_call | solution.py:321
  72.5 10.6 %all_to_all.27.shared_ref = f32[8,16,128]{2,1,0:T(8,128)S(1)} all-to-all(f32[8,16,128]{2,1,0:T(8,128)S(1)} %next_denominators.1), channel_id=1, replica_groups=mesh['win'=8,'frame'=64] {'win'}, dimensions={0} | all-to-all | bytes 131072 | tf_op jit(solution)/shard_map/all_to_all | solution.py:240
  83.2 2.2 %window_totals.3 = f32[64,4,128]{2,1,0:T(4,128)S(1)} custom-call(f32[8,16,128]{2,1,0:T(8,128)S(1)} %all_to_all.27.shared_ref, f32[512,1536]{1,0:T(8,128)S(1)} %get-tuple-element.12.near_ref, f32[16,128]{1,0:T(8,128)S(1)} %get-tuple-element.16.used_ref, f32[512,512]{1,0:T(8,128)S(1)} %get-tuple-element.17.far_ref), custom_call_target="tpu_custom_call" | custom-call | tf_op jit(solution)/shard_map/window_totals/pallas_call | solution.py:305
  85.4 19.1 %all_to_all.28 = f32[64,4,128]{2,1,0:T(4,128)S(1)} all-to-all(f32[64,4,128]{2,1,0:T(4,128)S(1)} %window_totals.3), channel_id=1, replica_groups=mesh['win'=8,'frame'=64] {'frame'}, dimensions={0} | all-to-all | bytes 262144 | tf_op jit(solution)/shard_map/all_to_all | solution.py:240
  104.5 0.1 reduce_max.9
  104.5 0.1 exponential_reduce_fusion
  104.6 0.6 multiply_bitcast_fusion
Async XLA Ops:
  1.7 34.0 %all-to-all-start = ((f32[64,4,128]{2,1,0:T(4,128)}), f32[64,4,128]{2,1,0:T(4,128)S(1)}, u32[]{:S(2)}, u32[]{:S(2)}) async-start(f32[64,4,128]{2,1,0:T(4,128)} %count_windows.1), calls=%async_computation | async-start | bytes 262144 | tf_op jit(solution)/shard_map/all_to_all | solution.py:240

commit v6 on v5

--- a/solution.py
+++ b/solution.py
@@ -17,6 +17,7 @@
 floor_value = -1e30
 log2_e = 1.0 / math.log(2.0)
 FAR = 1
+FIRST = {"frame": 34, "win": 4}
 least_sum = 2.0**-80
 most_sum = 2.0**100
 
@@ -237,7 +238,9 @@
 
 
 def exchange(copies, axis):
-    return lax.all_to_all(copies, axis, split_axis=0, concat_axis=0, tiled=True)
+    count = lax.axis_size(axis)
+    order = [(member + FIRST[axis]) % count for member in range(count)]
+    return lax.all_to_all(copies, axis, split_axis=0, concat_axis=0, tiled=True, axis_index_groups=[order])
 
 
 def on_device(distances, sample_ids, lengths, stiffness, centers):

time: 107 us -> 98.1 us (0.917); the launches traced: 105 us -> 97.7 us
  waiting for transfers between devices: 9.37 us -> 0.48 us
  starting transfers between devices: 19.1 us -> 22.9 us
  blocking collectives: 61.6 us -> 59.3 us
    all_to_all x1, waiting for transfers between devices: 9.37 us -> 0.48 us  [exchange(): lax.all_to_all(copies, axis, split_axis=0, concat_axis=0, tiled=True, axi...]
    all_to_all x1, starting transfers between devices: 19.1 us -> 22.9 us  [exchange(): lax.all_to_all(copies, axis, split_axis=0, concat_axis=0, tiled=True, axi...]
    all_to_all x4, blocking collectives: 61.6 us -> 59.3 us  [exchange(): lax.all_to_all(copies, axis, split_axis=0, concat_axis=0, tiled=True, axi...]
  transfers between devices with their start and end apart: 1 -> 1, of which waited for: 1 -> 1; matrix products, arithmetic and copies ran while one was open for 0% -> 0% of each run, Pallas kernels for 5% -> 6%
where the time goes in v6:
time: 98.1 us; the launch traced here: 97.7 us
  blocking collectives  59.3 us (60%)
  starting transfers between devices  22.9 us (23%)
  Pallas kernels  14.3 us (15%)
    all_to_all x4, blocking collectives, exchange(): lax.all_to_all(copies, axis, split_axis=0, concat_axis=0, tiled=True, axi...  59.3 us
    all_to_all x1, starting transfers between devices, exchange(): lax.all_to_all(copies, axis, split_axis=0, concat_axis=0, tiled=True, axi...  22.9 us
    pallas_call x1, Pallas kernels, on_device(): pl.pallas_call(energy_kernel, out_shape=(near_shape, tops_shape, pltpu.HB...  5.52 us
    pallas_call x2, Pallas kernels, on_device(): pl.pallas_call(window_kernel, out_shape=to_frame, in_specs=[in_vmem] * 4,...  4.44 us
  transfers between devices with their start and end apart: 1, of which 1 were waited for; matrix products, arithmetic and copies ran while one was open for 0% of the time, Pallas kernels for 6%

profile of v6, /device:TPU:1, one launch (start us, length us, event | category | flops | bytes accessed | tf_op | source)
XLA Modules:
  0.0 97.7 jit_solution(15655317586677080037)
XLA Ops:
  0.0 1.6 %count_windows.1 = f32[64,4,128]{2,1,0:T(4,128)} custom-call(s32[64]{0:T(128)} %lengths_hbm.3, s32[1,2048]{1,0:T(1,128)} %bitcast.5), custom_call_target="tpu_custom_call" | custom-call | tf_op jit(solution)/shard_map/count_windows/pallas_call | solution.py:253
  1.7 22.9 %all-to-all-start = ((f32[64,4,128]{2,1,0:T(4,128)}), f32[64,4,128]{2,1,0:T(4,128)S(1)}, u32[]{:S(2)}, u32[]{:S(2)}) async-start(f32[64,4,128]{2,1,0:T(4,128)} %count_windows.1), calls=%async_computation | async-start | bytes 262144 | tf_op jit(solution)/shard_map/all_to_all | solution.py:243
  24.5 5.5 %energies.1 = (f32[512,1536]{1,0:T(8,128)S(1)}, f32[16,128]{1,0:T(8,128)S(1)}, f32[512,512]{1,0:T(8,128)}) custom-call(f32[32,512]{1,0:T(8,128)} %bitcast.6, f32[32,512]{1,0:T(8,128)} %bitcast.7, f32[32,2048]{1,0:T(8,128)} %distances_hbm.1), custom_call_target="tpu_custom_call" | custom-call | flops 805306368 | bytes 4194304 | tf_op jit(solution)/shard_map/energies/pallas_call | solution.py:272
  30.0 0.5 all-to-all-done.shared_ref
  30.5 1.6 %first_denominators.1 = (f32[4,128]{1,0:T(4,128)S(1)}, f32[8,16,128]{2,1,0:T(8,128)S(1)}, f32[512,512]{1,0:T(8,128)S(1)}, f32[16,128]{1,0:T(8,128)S(1)}) custom-call(s32[64]{0:T(128)} %lengths_hbm.3, f32[64,4,128]{2,1,0:T(4,128)S(1)} %all-to-all-done.shared_ref, f32[512,1536]{1,0:T(8,128)S(1)} %get-tuple-element.12.near_ref, ...), custom_call_target="tpu_custom_call" | custom-call | tf_op jit(solution)/shard_map/first_denominators/pallas_call | solution.py:298
  32.1 8.9 %all_to_all.25.shared_ref = f32[8,16,128]{2,1,0:T(8,128)S(1)} all-to-all(f32[8,16,128]{2,1,0:T(8,128)S(1)} %get-tuple-element.15), channel_id=1, replica_groups={{256,320,384,448,0,64,128,192},{257,321,385,449,1,65,129,193},{258,322,..., dimensions={0} | all-to-all | bytes 131072 | tf_op jit(solution)/shard_map/all_to_all | solution.py:243
  41.0 2.2 %window_totals.2 = f32[64,4,128]{2,1,0:T(4,128)S(1)} custom-call(f32[8,16,128]{2,1,0:T(8,128)S(1)} %all_to_all.25.shared_ref, f32[512,1536]{1,0:T(8,128)S(1)} %get-tuple-element.12.near_ref, f32[16,128]{1,0:T(8,128)S(1)} %get-tuple-element.16.used_ref, f32[512,512]{1,0:T(8,128)S(1)} %get-tuple-element.17.far_ref), custom_call_target="tpu_custom_call" | custom-call | tf_op jit(solution)/shard_map/window_totals/pallas_call | solution.py:308
  43.3 20.8 %all_to_all.26.shared_ref = f32[64,4,128]{2,1,0:T(4,128)S(1)} all-to-all(f32[64,4,128]{2,1,0:T(4,128)S(1)} %window_totals.2), channel_id=1, replica_groups={{34,35,36,37,38,39,40,41,42,43,44,45,46,47,48,49,50,51,52,53,54,55,56,5..., dimensions={0} | all-to-all | bytes 262144 | tf_op jit(solution)/shard_map/all_to_all | solution.py:243
  64.1 1.1 %next_denominators.1 = f32[8,16,128]{2,1,0:T(8,128)S(1)} custom-call(f32[64,4,128]{2,1,0:T(4,128)S(1)} %all_to_all.26.shared_ref, f32[4,128]{1,0:T(4,128)S(1)} %get-tuple-element.18.counts_ref, f32[512,1536]{1,0:T(8,128)S(1)} %get-tuple-element.12.near_ref, f32[16,128]{1,0:T(8,128)S(1)} %get-tuple-element.13.tops_ref, f32[512,512]{1,0:T(8,128)S(1)} %get-tuple-element.17.far_ref), custom_call_target="tpu_custom_call" | custom-call | tf_op jit(solution)/shard_map/next_denominators/pallas_call | solution.py:324
  65.2 8.7 %all_to_all.27.shared_ref = f32[8,16,128]{2,1,0:T(8,128)S(1)} all-to-all(f32[8,16,128]{2,1,0:T(8,128)S(1)} %next_denominators.1), channel_id=1, replica_groups={{256,320,384,448,0,64,128,192},{257,321,385,449,1,65,129,193},{258,322,..., dimensions={0} | all-to-all | bytes 131072 | tf_op jit(solution)/shard_map/all_to_all | solution.py:243
  73.9 2.2 %window_totals.3 = f32[64,4,128]{2,1,0:T(4,128)S(1)} custom-call(f32[8,16,128]{2,1,0:T(8,128)S(1)} %all_to_all.27.shared_ref, f32[512,1536]{1,0:T(8,128)S(1)} %get-tuple-element.12.near_ref, f32[16,128]{1,0:T(8,128)S(1)} %get-tuple-element.16.used_ref, f32[512,512]{1,0:T(8,128)S(1)} %get-tuple-element.17.far_ref), custom_call_target="tpu_custom_call" | custom-call | tf_op jit(solution)/shard_map/window_totals/pallas_call | solution.py:308
  76.1 20.8 %all_to_all.28 = f32[64,4,128]{2,1,0:T(4,128)S(1)} all-to-all(f32[64,4,128]{2,1,0:T(4,128)S(1)} %window_totals.3), channel_id=1, replica_groups={{34,35,36,37,38,39,40,41,42,43,44,45,46,47,48,49,50,51,52,53,54,55,56,5..., dimensions={0} | all-to-all | bytes 262144 | tf_op jit(solution)/shard_map/all_to_all | solution.py:243
  96.9 0.1 reduce_max.9
  97.0 0.1 exponential_reduce_fusion
  97.1 0.6 multiply_bitcast_fusion
Async XLA Ops:
  1.7 28.9 %all-to-all-start = ((f32[64,4,128]{2,1,0:T(4,128)}), f32[64,4,128]{2,1,0:T(4,128)S(1)}, u32[]{:S(2)}, u32[]{:S(2)}) async-start(f32[64,4,128]{2,1,0:T(4,128)} %count_windows.1), calls=%async_computation | async-start | bytes 262144 | tf_op jit(solution)/shard_map/all_to_all | solution.py:243

commit v7 on v6

--- a/solution.py
+++ b/solution.py
@@ -16,7 +16,7 @@
 
 floor_value = -1e30
 log2_e = 1.0 / math.log(2.0)
-FAR = 1
+FAR = 384
 FIRST = {"frame": 34, "win": 4}
 least_sum = 2.0**-80
 most_sum = 2.0**100
@@ -88,30 +88,33 @@
     first = lax.broadcasted_iota(jnp.int32, (8, constant.shape[1]), 0) == 0
     constant_rows = jnp.where(first, jnp.broadcast_to(constant, first.shape), 0.0)
     coef_rows = jnp.concatenate([stiffness * centers, -0.5 * stiffness, constant_rows], axis=0).T
-    unit_rows = jnp.where(lax.broadcasted_iota(jnp.int32, (8, STEP), 0) == 0, 1.0, 0.0)
-
-    def one(step, to_ref, to):
-        start = pl.multiple_of(step * STEP, STEP)
-        separations = distances_ref[:, pl.ds(start, STEP)]
+
+    def one(start, size, to_ref, to):
+        unit_rows = jnp.where(lax.broadcasted_iota(jnp.int32, (8, size), 0) == 0, 1.0, 0.0)
+        separations = distances_ref[:, pl.ds(start, size)]
         features = jnp.concatenate([separations, separations * separations, unit_rows], axis=0)
         exponents = jnp.dot(
             coef_rows, features, precision=lax.Precision.HIGHEST, preferred_element_type=jnp.float32
         )
         top = jnp.max(exponents, axis=0, keepdims=True)
-        to_ref[:, pl.ds(to, STEP)] = exponents - top
-        for part in range(STEP // LANES):
-            tops_ref[pl.ds(step * (STEP // LANES) + part, 1), :] = top[:, part * LANES : (part + 1) * LANES]
-
-    near_steps = near_ref.shape[1] // STEP
+        to_ref[:, pl.ds(to, size)] = exponents - top
+        for part in range(size // LANES):
+            tops_ref[pl.ds(start // LANES + part, 1), :] = top[:, part * LANES : (part + 1) * LANES]
+
+    near_frames, far_frames = near_ref.shape[1], far_ref.shape[1]
     copy = pltpu.make_async_copy(far_ref, far_hbm, far_sem)
-    one(near_steps, far_ref, 0)
+    one(near_frames, far_frames, far_ref, 0)
     copy.start()
 
     def near(step, carry):
-        one(step, near_ref, pl.multiple_of(step * STEP, STEP))
+        start = pl.multiple_of(step * STEP, STEP)
+        one(start, STEP, near_ref, start)
         return carry
 
-    lax.fori_loop(0, near_steps, near, 0)
+    lax.fori_loop(0, near_frames // STEP, near, 0)
+    rest = near_frames % STEP
+    if rest:
+        one(near_frames - rest, rest, near_ref, near_frames - rest)
     copy.wait()
 
 
@@ -237,6 +240,10 @@
         out_ref[...] = jnp.broadcast_to(row_ref[...][None], out_ref.shape)
 
 
+def last_kernel(shared_ref, out_ref):
+    out_ref[...] = -math.log(2.0) * log2_sum(shared_ref[...])
+
+
 def exchange(copies, axis):
     count = lax.axis_size(axis)
     order = [(member + FIRST[axis]) % count for member in range(count)]
@@ -245,7 +252,7 @@
 
 def on_device(distances, sample_ids, lengths, stiffness, centers):
     windows, capacity = stiffness.shape[0], distances.shape[1]
-    groups, blocks, steps = windows // LANES, capacity // LANES, capacity // STEP
+    groups, blocks = windows // LANES, capacity // LANES
     f32, dma = jnp.float32, pltpu.SemaphoreType.DMA
     to_frame = jax.ShapeDtypeStruct((lax.axis_size("frame"), groups, LANES), f32)
     to_win = jax.ShapeDtypeStruct((lax.axis_size("win"), blocks, LANES), f32)
@@ -265,9 +272,8 @@
         name="count_windows",
     )(lengths, sample_ids.reshape(1, capacity))
     shared = exchange(local_counts, "frame")
-    far_frames = FAR * STEP
-    near_shape = jax.ShapeDtypeStruct((windows, capacity - far_frames), f32)
-    far_shape = jax.ShapeDtypeStruct((windows, far_frames), f32)
+    near_shape = jax.ShapeDtypeStruct((windows, capacity - FAR), f32)
+    far_shape = jax.ShapeDtypeStruct((windows, FAR), f32)
     tops_shape = jax.ShapeDtypeStruct((blocks, LANES), f32)
     near, tops, far = pl.pallas_call(
         energy_kernel,
@@ -330,7 +336,15 @@
                 compiler_params=grant,
                 name="next_denominators",
             )(shared, counts, near, tops, far)
-    return (-math.log(2.0) * log2_sum(shared)).reshape(windows)
+    free_energy = pl.pallas_call(
+        last_kernel,
+        out_shape=jax.ShapeDtypeStruct((groups, LANES), f32),
+        in_specs=[in_vmem],
+        out_specs=in_vmem,
+        compiler_params=grant,
+        name="free_energies",
+    )(shared)
+    return free_energy.reshape(windows)
 
 
 def solution(mesh):

time: 98.1 us -> 97.8 us (level)
  no operation moved by 1% of the time
where the time goes in v7:
time: 97.8 us; the launch traced here: 97.4 us
  blocking collectives  59.3 us (61%)
  starting transfers between devices  22.9 us (23%)
  Pallas kernels  14.7 us (15%)
    all_to_all x4, blocking collectives, exchange(): lax.all_to_all(copies, axis, split_axis=0, concat_axis=0, tiled=True, axi...  59.3 us
    all_to_all x1, starting transfers between devices, exchange(): lax.all_to_all(copies, axis, split_axis=0, concat_axis=0, tiled=True, axi...  22.9 us
    pallas_call x1, Pallas kernels, on_device(): pl.pallas_call(energy_kernel, out_shape=(near_shape, tops_shape, pltpu.HB...  5.45 us
    pallas_call x2, Pallas kernels, on_device(): pl.pallas_call(window_kernel, out_shape=to_frame, in_specs=[in_vmem] * 4,...  4.43 us
  transfers between devices with their start and end apart: 1, of which 1 were waited for; matrix products, arithmetic and copies ran while one was open for 0% of the time, Pallas kernels for 6%

profile of v7, /device:TPU:1, one launch (start us, length us, event | category | flops | bytes accessed | tf_op | source)
XLA Modules:
  0.0 97.4 jit_solution(13324700875245331591)
XLA Ops:
  0.0 1.6 %count_windows.1 = f32[64,4,128]{2,1,0:T(4,128)} custom-call(s32[64]{0:T(128)} %lengths_hbm.3, s32[1,2048]{1,0:T(1,128)} %bitcast.4), custom_call_target="tpu_custom_call" | custom-call | tf_op jit(solution)/shard_map/count_windows/pallas_call | solution.py:260
  1.7 22.9 %all-to-all-start = ((f32[64,4,128]{2,1,0:T(4,128)}), f32[64,4,128]{2,1,0:T(4,128)S(1)}, u32[]{:S(2)}, u32[]{:S(2)}) async-start(f32[64,4,128]{2,1,0:T(4,128)} %count_windows.1), calls=%async_computation | async-start | bytes 262144 | tf_op jit(solution)/shard_map/all_to_all | solution.py:250
  24.5 5.4 %energies.1 = (f32[512,1664]{1,0:T(8,128)S(1)}, f32[16,128]{1,0:T(8,128)S(1)}, f32[512,384]{1,0:T(8,128)}) custom-call(f32[32,512]{1,0:T(8,128)} %bitcast.5, f32[32,512]{1,0:T(8,128)} %bitcast.6, f32[32,2048]{1,0:T(8,128)} %distances_hbm.1), custom_call_target="tpu_custom_call" | custom-call | flops 805306368 | bytes 4194304 | tf_op jit(solution)/shard_map/energies/pallas_call | solution.py:278
  30.0 0.6 all-to-all-done.shared_ref
  30.5 1.4 %first_denominators.1 = (f32[4,128]{1,0:T(4,128)S(1)}, f32[8,16,128]{2,1,0:T(8,128)S(1)}, f32[512,384]{1,0:T(8,128)S(1)}, f32[16,128]{1,0:T(8,128)S(1)}) custom-call(s32[64]{0:T(128)} %lengths_hbm.3, f32[64,4,128]{2,1,0:T(4,128)S(1)} %all-to-all-done.shared_ref, f32[512,1664]{1,0:T(8,128)S(1)} %get-tuple-element.12.near_ref, ...), custom_call_target="tpu_custom_call" | custom-call | tf_op jit(solution)/shard_map/first_denominators/pallas_call | solution.py:304
  32.0 8.9 %all_to_all.25.shared_ref = f32[8,16,128]{2,1,0:T(8,128)S(1)} all-to-all(f32[8,16,128]{2,1,0:T(8,128)S(1)} %get-tuple-element.15), channel_id=1, replica_groups={{256,320,384,448,0,64,128,192},{257,321,385,449,1,65,129,193},{258,322,..., dimensions={0} | all-to-all | bytes 131072 | tf_op jit(solution)/shard_map/all_to_all | solution.py:250
  40.9 2.2 %window_totals.2 = f32[64,4,128]{2,1,0:T(4,128)S(1)} custom-call(f32[8,16,128]{2,1,0:T(8,128)S(1)} %all_to_all.25.shared_ref, f32[512,1664]{1,0:T(8,128)S(1)} %get-tuple-element.12.near_ref, f32[16,128]{1,0:T(8,128)S(1)} %get-tuple-element.16.used_ref, f32[512,384]{1,0:T(8,128)S(1)} %get-tuple-element.17.far_ref), custom_call_target="tpu_custom_call" | custom-call | tf_op jit(solution)/shard_map/window_totals/pallas_call | solution.py:314
  43.1 20.8 %all_to_all.26.shared_ref = f32[64,4,128]{2,1,0:T(4,128)S(1)} all-to-all(f32[64,4,128]{2,1,0:T(4,128)S(1)} %window_totals.2), channel_id=1, replica_groups={{34,35,36,37,38,39,40,41,42,43,44,45,46,47,48,49,50,51,52,53,54,55,56,5..., dimensions={0} | all-to-all | bytes 262144 | tf_op jit(solution)/shard_map/all_to_all | solution.py:250
  63.9 1.0 %next_denominators.1 = f32[8,16,128]{2,1,0:T(8,128)S(1)} custom-call(f32[64,4,128]{2,1,0:T(4,128)S(1)} %all_to_all.26.shared_ref, f32[4,128]{1,0:T(4,128)S(1)} %get-tuple-element.18.counts_ref, f32[512,1664]{1,0:T(8,128)S(1)} %get-tuple-element.12.near_ref, f32[16,128]{1,0:T(8,128)S(1)} %get-tuple-element.13.tops_ref, f32[512,384]{1,0:T(8,128)S(1)} %get-tuple-element.17.far_ref), custom_call_target="tpu_custom_call" | custom-call | tf_op jit(solution)/shard_map/next_denominators/pallas_call | solution.py:330
  65.0 8.7 %all_to_all.27.shared_ref = f32[8,16,128]{2,1,0:T(8,128)S(1)} all-to-all(f32[8,16,128]{2,1,0:T(8,128)S(1)} %next_denominators.1), channel_id=1, replica_groups={{256,320,384,448,0,64,128,192},{257,321,385,449,1,65,129,193},{258,322,..., dimensions={0} | all-to-all | bytes 131072 | tf_op jit(solution)/shard_map/all_to_all | solution.py:250
  73.7 2.2 %window_totals.3 = f32[64,4,128]{2,1,0:T(4,128)S(1)} custom-call(f32[8,16,128]{2,1,0:T(8,128)S(1)} %all_to_all.27.shared_ref, f32[512,1664]{1,0:T(8,128)S(1)} %get-tuple-element.12.near_ref, f32[16,128]{1,0:T(8,128)S(1)} %get-tuple-element.16.used_ref, f32[512,384]{1,0:T(8,128)S(1)} %get-tuple-element.17.far_ref), custom_call_target="tpu_custom_call" | custom-call | tf_op jit(solution)/shard_map/window_totals/pallas_call | solution.py:314
  75.9 20.8 %all_to_all.28.shared_ref = f32[64,4,128]{2,1,0:T(4,128)S(1)} all-to-all(f32[64,4,128]{2,1,0:T(4,128)S(1)} %window_totals.3), channel_id=1, replica_groups={{34,35,36,37,38,39,40,41,42,43,44,45,46,47,48,49,50,51,52,53,54,55,56,5..., dimensions={0} | all-to-all | bytes 262144 | tf_op jit(solution)/shard_map/all_to_all | solution.py:250
  96.8 0.7 free_energies.1
Async XLA Ops:
  1.7 28.9 %all-to-all-start = ((f32[64,4,128]{2,1,0:T(4,128)}), f32[64,4,128]{2,1,0:T(4,128)S(1)}, u32[]{:S(2)}, u32[]{:S(2)}) async-start(f32[64,4,128]{2,1,0:T(4,128)} %count_windows.1), calls=%async_computation | async-start | bytes 262144 | tf_op jit(solution)/shard_map/all_to_all | solution.py:250

commit v8 on v7

--- a/solution.py
+++ b/solution.py
@@ -18,8 +18,8 @@
 log2_e = 1.0 / math.log(2.0)
 FAR = 384
 FIRST = {"frame": 34, "win": 4}
-least_sum = 2.0**-80
-most_sum = 2.0**100
+least_sum = 2.0**-85
+most_rate = 2.0**99
 
 in_vmem = pl.BlockSpec(memory_space=pltpu.VMEM)
 in_hbm = pl.BlockSpec(memory_space=pltpu.HBM)
@@ -72,8 +72,8 @@
 
 
 def energy_kernel(
-    stiffness_hbm, centers_hbm, distances_hbm, near_ref, tops_ref, far_hbm,
-    stiffness_ref, centers_ref, distances_ref, far_ref, in_sems, far_sem,
+    stiffness_hbm, centers_hbm, distances_hbm, near_ref, tops_ref, far_hbm, fall_hbm,
+    stiffness_ref, centers_ref, distances_ref, far_ref, fall_ref, in_sems, far_sem, fall_sems,
 ):
     together(
         [
@@ -89,7 +89,11 @@
     constant_rows = jnp.where(first, jnp.broadcast_to(constant, first.shape), 0.0)
     coef_rows = jnp.concatenate([stiffness * centers, -0.5 * stiffness, constant_rows], axis=0).T
 
-    def one(start, size, to_ref, to):
+    def send(index, start, size):
+        columns = pl.ds(start, size)
+        return pltpu.make_async_copy(fall_ref.at[:, columns], fall_hbm.at[:, columns], fall_sems.at[index])
+
+    def one(index, start, size, to_ref, to):
         unit_rows = jnp.where(lax.broadcasted_iota(jnp.int32, (8, size), 0) == 0, 1.0, 0.0)
         separations = distances_ref[:, pl.ds(start, size)]
         features = jnp.concatenate([separations, separations * separations, unit_rows], axis=0)
@@ -97,40 +101,52 @@
             coef_rows, features, precision=lax.Precision.HIGHEST, preferred_element_type=jnp.float32
         )
         top = jnp.max(exponents, axis=0, keepdims=True)
-        to_ref[:, pl.ds(to, size)] = exponents - top
+        fall = exponents - top
+        fall_ref[:, pl.ds(start, size)] = fall
+        send(index, start, size).start()
+        to_ref[:, pl.ds(to, size)] = jnp.exp2(fall)
         for part in range(size // LANES):
             tops_ref[pl.ds(start // LANES + part, 1), :] = top[:, part * LANES : (part + 1) * LANES]
 
     near_frames, far_frames = near_ref.shape[1], far_ref.shape[1]
     copy = pltpu.make_async_copy(far_ref, far_hbm, far_sem)
-    one(near_frames, far_frames, far_ref, 0)
+    steps, rest = near_frames // STEP, near_frames % STEP
+    one(steps, near_frames, far_frames, far_ref, 0)
     copy.start()
 
     def near(step, carry):
         start = pl.multiple_of(step * STEP, STEP)
-        one(start, STEP, near_ref, start)
+        one(step, start, STEP, near_ref, start)
         return carry
 
-    lax.fori_loop(0, near_frames // STEP, near, 0)
-    rest = near_frames % STEP
+    lax.fori_loop(0, steps, near, 0)
     if rest:
-        one(near_frames - rest, rest, near_ref, near_frames - rest)
+        one(steps + 1, near_frames - rest, rest, near_ref, near_frames - rest)
+        send(steps + 1, near_frames - rest, rest).wait()
     copy.wait()
-
-
-def denominators(shifted, arrive, parts, tops_ref, out_ref, column_ref, part_ref, row_ref):
-    groups = shifted.shape[0]
+    send(steps, near_frames, far_frames).wait()
+    for step in range(steps):
+        send(step, step * STEP, STEP).wait()
+
+
+def spread(row, to_ref):
+    for group in range(row.shape[0]):
+        lanes = jnp.broadcast_to(row[group : group + 1], (LANES, LANES))
+        to_ref[group * LANES : (group + 1) * LANES, :] = lanes.T
+
+
+def denominators(shifted, arrive, parts, fall_hbm, tops_ref, out_ref, scratch):
+    column_ref, part_ref, row_ref, fall_ref, fall_sem = scratch
     most = jnp.max(jnp.max(shifted, axis=0, keepdims=True), axis=1, keepdims=True)
-    for group in range(groups):
-        spread = jnp.broadcast_to(shifted[group : group + 1] - most, (LANES, LANES))
-        column_ref[group * LANES : (group + 1) * LANES, :] = spread.T
+    spread(jnp.exp2(shifted - most), column_ref)
     windows = column_ref.shape[0]
     chunks = [slice(start, start + ROWS) for start in range(0, windows, ROWS)]
 
-    def exponents(ref, rows, block):
-        return (ref[rows, pl.ds(pl.multiple_of(block * LANES, LANES), LANES)] + column_ref[rows, :]).reshape(
-            -1, 8, LANES
-        )
+    def columns(block):
+        return pl.ds(pl.multiple_of(block * LANES, LANES), LANES)
+
+    def fold(values):
+        return values.reshape(-1, 8, LANES)
 
     done = 0
     for part, ref in enumerate(parts):
@@ -139,7 +155,7 @@
         count = ref.shape[1] // LANES
 
         def one(block, carry, ref=ref, done=done):
-            sums = [jnp.sum(jnp.exp2(exponents(ref, rows, block)), axis=0) for rows in chunks]
+            sums = [jnp.sum(fold(ref[rows, columns(block)] * column_ref[rows, :]), axis=0) for rows in chunks]
             part_ref[done + block] = functools.reduce(jnp.add, sums)
             return carry
 
@@ -150,26 +166,29 @@
 
     @pl.when(jnp.min(totals) < least_sum)
     def _():
-        done = 0
-        for ref in parts:
-            count = ref.shape[1] // LANES
-
-            def exact(block, carry, ref=ref, done=done):
-                tops = [jnp.max(exponents(ref, rows, block), axis=0) for rows in chunks]
-                highest = jnp.max(functools.reduce(jnp.maximum, tops), axis=0, keepdims=True)
-                sums = [jnp.sum(jnp.exp2(exponents(ref, rows, block) - highest), axis=0) for rows in chunks]
-                total = jnp.sum(functools.reduce(jnp.add, sums), axis=0, keepdims=True)
-                row_ref[pl.ds(done + block, 1), :] = highest + log2(total)
-                return carry
-
-            lax.fori_loop(0, count, exact, 0)
-            done += count
+        copy = pltpu.make_async_copy(fall_hbm, fall_ref, fall_sem)
+        copy.start()
+        spread(shifted - most, column_ref)
+        copy.wait()
+
+        def exponents(rows, block):
+            return fold(fall_ref[rows, columns(block)] + column_ref[rows, :])
+
+        def exact(block, carry):
+            tops = [jnp.max(exponents(rows, block), axis=0) for rows in chunks]
+            highest = jnp.max(functools.reduce(jnp.maximum, tops), axis=0, keepdims=True)
+            sums = [jnp.sum(jnp.exp2(exponents(rows, block) - highest), axis=0) for rows in chunks]
+            total = jnp.sum(functools.reduce(jnp.add, sums), axis=0, keepdims=True)
+            row_ref[pl.ds(block, 1), :] = highest + log2(total)
+            return carry
+
+        lax.fori_loop(0, row_ref.shape[0], exact, 0)
         out_ref[...] = jnp.broadcast_to((tops_ref[...] + most + row_ref[...])[None], out_ref.shape)
 
 
 def first_kernel(
-    lengths_hbm, shared_ref, near_ref, tops_ref, far_hbm, counts_ref, out_ref, far_ref, used_ref,
-    column_ref, part_ref, row_ref, lengths_ref, sem, lengths_sem,
+    lengths_hbm, shared_ref, near_ref, tops_ref, far_hbm, fall_hbm, counts_ref, out_ref, far_ref, used_ref,
+    lengths_ref, sem, lengths_sem, *scratch,
 ):
     copy = pltpu.make_async_copy(far_hbm, far_ref, sem)
     lengths_copy = pltpu.make_async_copy(lengths_hbm, lengths_ref, lengths_sem)
@@ -178,7 +197,7 @@
     counts = jnp.sum(shared_ref[...], axis=0)
     counts_ref[...] = counts
     shifted = jnp.where(counts > 0.5, log2(jnp.maximum(counts, 1.0)), floor_value)
-    denominators(shifted, copy.wait, (near_ref, far_ref), tops_ref, out_ref, column_ref, part_ref, row_ref)
+    denominators(shifted, copy.wait, (near_ref, far_ref), fall_hbm, tops_ref, out_ref, scratch)
     lengths_copy.wait()
     own_length = lengths_ref[lax.axis_index("frame")]
     slots = (
@@ -188,27 +207,35 @@
     used_ref[...] = jnp.where(slots < own_length, tops_ref[...], floor_value)
 
 
-def next_kernel(shared_ref, counts_ref, near_ref, tops_ref, far_ref, out_ref, column_ref, part_ref, row_ref):
+def next_kernel(shared_ref, counts_ref, near_ref, tops_ref, far_ref, fall_hbm, out_ref, *scratch):
     counts = counts_ref[...]
     free_energy = -log2_sum(shared_ref[...])
     shifted = jnp.where(counts > 0.5, log2(jnp.maximum(counts, 1.0)) + free_energy, floor_value)
-    denominators(shifted, lambda: None, (near_ref, far_ref), tops_ref, out_ref, column_ref, part_ref, row_ref)
-
-
-def window_kernel(shared_ref, near_ref, used_ref, far_ref, out_ref, den_ref, top_ref, sum_ref, row_ref):
-    windows, near_blocks, far_blocks = near_ref.shape[0], near_ref.shape[1] // LANES, far_ref.shape[1] // LANES
+    denominators(shifted, lambda: None, (near_ref, far_ref), fall_hbm, tops_ref, out_ref, scratch)
+
+
+def window_kernel(
+    shared_ref, near_ref, used_ref, far_ref, fall_hbm, out_ref, den_ref, rate_ref, top_ref, sum_ref, row_ref, fall_ref, fall_sem
+):
+    windows, blocks = near_ref.shape[0], den_ref.shape[0]
     groups = windows // LANES
-    den_ref[...] = log2_sum(shared_ref[...]) - used_ref[...]
-
-    def exponents(chunk):
-        rows = pl.ds(pl.multiple_of(chunk * ROWS, ROWS), ROWS)
-        for ref, done in ((near_ref, 0), (far_ref, near_blocks)):
-            for block in range(ref.shape[1] // LANES):
-                yield ref[rows, block * LANES : (block + 1) * LANES] - den_ref[done + block : done + block + 1, :]
+    den = log2_sum(shared_ref[...]) - used_ref[...]
+    den_ref[...] = den
+    rates = jnp.exp2(-jnp.maximum(den, -100.0))
+    rate_ref[...] = rates
+    fastest = jnp.max(rates)
+
+    def rows_of(chunk):
+        return pl.ds(pl.multiple_of(chunk * ROWS, ROWS), ROWS)
 
     def one(chunk, carry):
-        rows = pl.ds(pl.multiple_of(chunk * ROWS, ROWS), ROWS)
-        sum_ref[rows, :] = functools.reduce(jnp.add, (jnp.exp2(each) for each in exponents(chunk)))
+        rows = rows_of(chunk)
+        terms = (
+            ref[rows, block * LANES : (block + 1) * LANES] * rate_ref[done + block : done + block + 1, :]
+            for ref, done in ((near_ref, 0), (far_ref, near_ref.shape[1] // LANES))
+            for block in range(ref.shape[1] // LANES)
+        )
+        sum_ref[rows, :] = functools.reduce(jnp.add, terms)
         return carry
 
     lax.fori_loop(0, windows // ROWS, one, 0)
@@ -219,15 +246,24 @@
         row_ref[group : group + 1, :] = log2(total)
     out_ref[...] = jnp.broadcast_to(row_ref[...][None], out_ref.shape)
     lowest = jnp.min(functools.reduce(jnp.minimum, totals))
-    highest = jnp.max(functools.reduce(jnp.maximum, totals))
-
-    @pl.when(jnp.logical_not(jnp.logical_and(lowest > least_sum, highest < most_sum)))
+    in_range = jnp.logical_and(lowest > least_sum * jnp.maximum(fastest, 1.0), fastest < most_rate)
+
+    @pl.when(jnp.logical_not(in_range))
     def _():
+        copy = pltpu.make_async_copy(fall_hbm, fall_ref, fall_sem)
+        copy.start()
+        copy.wait()
+
+        def exponents(rows, block):
+            return fall_ref[rows, block * LANES : (block + 1) * LANES] - den_ref[block : block + 1, :]
+
         def exact(chunk, carry):
-            rows = pl.ds(pl.multiple_of(chunk * ROWS, ROWS), ROWS)
-            top = functools.reduce(jnp.maximum, exponents(chunk))
+            rows = rows_of(chunk)
+            top = functools.reduce(jnp.maximum, (exponents(rows, block) for block in range(blocks)))
             top_ref[rows, :] = top
-            sum_ref[rows, :] = functools.reduce(jnp.add, (jnp.exp2(each - top) for each in exponents(chunk)))
+            sum_ref[rows, :] = functools.reduce(
+                jnp.add, (jnp.exp2(exponents(rows, block) - top) for block in range(blocks))
+            )
             return carry
 
         lax.fori_loop(0, windows // ROWS, exact, 0)
@@ -275,18 +311,26 @@
     near_shape = jax.ShapeDtypeStruct((windows, capacity - FAR), f32)
     far_shape = jax.ShapeDtypeStruct((windows, FAR), f32)
     tops_shape = jax.ShapeDtypeStruct((blocks, LANES), f32)
-    near, tops, far = pl.pallas_call(
+    fall_here = [pltpu.VMEM((windows, capacity), f32), dma]
+    near, tops, far, fall = pl.pallas_call(
         energy_kernel,
-        out_shape=(near_shape, tops_shape, pltpu.HBM(far_shape.shape, f32)),
+        out_shape=(
+            near_shape,
+            tops_shape,
+            pltpu.HBM(far_shape.shape, f32),
+            pltpu.HBM((windows, capacity), f32),
+        ),
         in_specs=[in_hbm] * 3,
-        out_specs=(in_vmem, in_vmem, in_hbm),
+        out_specs=(in_vmem, in_vmem, in_hbm, in_hbm),
         scratch_shapes=[
             pltpu.VMEM((stiffness.shape[1], windows), f32),
             pltpu.VMEM((stiffness.shape[1], windows), f32),
             pltpu.VMEM(distances.shape, f32),
             pltpu.VMEM(far_shape.shape, f32),
+            pltpu.VMEM((windows, capacity), f32),
             dma((3,)),
             dma,
+            dma((capacity // STEP + 1,)),
         ],
         compiler_params=grant,
         cost_estimate=pl.CostEstimate(
@@ -296,46 +340,50 @@
         ),
         name="energies",
     )(hbm(stiffness.T), hbm(centers.T), hbm(distances))
+    fall = hbm(fall)
     den_scratch = [
         pltpu.VMEM((windows, LANES), f32),
         pltpu.VMEM((blocks, 8, LANES), f32),
         pltpu.VMEM((blocks, LANES), f32),
+        *fall_here,
     ]
     counts, own_den, far, used = pl.pallas_call(
         first_kernel,
         out_shape=(jax.ShapeDtypeStruct((groups, LANES), f32), to_win, far_shape, tops_shape),
-        in_specs=[in_hbm, in_vmem, in_vmem, in_vmem, in_hbm],
+        in_specs=[in_hbm, in_vmem, in_vmem, in_vmem, in_hbm, in_hbm],
         out_specs=(in_vmem,) * 4,
-        scratch_shapes=[*den_scratch, lengths_here, dma, dma],
+        scratch_shapes=[lengths_here, dma, dma, *den_scratch],
         compiler_params=grant,
         name="first_denominators",
-    )(hbm(lengths), shared, near, tops, hbm(far))
+    )(hbm(lengths), shared, near, tops, hbm(far), fall)
     for iteration in range(ITERS):
         own_total = pl.pallas_call(
             window_kernel,
             out_shape=to_frame,
-            in_specs=[in_vmem] * 4,
+            in_specs=[in_vmem] * 4 + [in_hbm],
             out_specs=in_vmem,
             scratch_shapes=[
+                pltpu.VMEM((blocks, LANES), f32),
                 pltpu.VMEM((blocks, LANES), f32),
                 pltpu.VMEM((windows, LANES), f32),
                 pltpu.VMEM((windows, LANES), f32),
                 pltpu.VMEM((groups, LANES), f32),
+                *fall_here,
             ],
             compiler_params=grant,
             name="window_totals",
-        )(exchange(own_den, "win"), near, used, far)
+        )(exchange(own_den, "win"), near, used, far, fall)
         shared = exchange(own_total, "frame")
         if iteration < ITERS - 1:
             own_den = pl.pallas_call(
                 next_kernel,
                 out_shape=to_win,
-                in_specs=[in_vmem] * 5,
+                in_specs=[in_vmem] * 5 + [in_hbm],
                 out_specs=in_vmem,
                 scratch_shapes=den_scratch,
                 compiler_params=grant,
                 name="next_denominators",
-            )(shared, counts, near, tops, far)
+            )(shared, counts, near, tops, far, fall)
     free_energy = pl.pallas_call(
         last_kernel,
         out_shape=jax.ShapeDtypeStruct((groups, LANES), f32),

time: 97.8 us -> 102 us (1.043)
  Pallas kernels: 14.7 us -> 19.9 us
    pallas_call x3, Pallas kernels: 5.48 us -> 9.17 us  [the longest x2 8.45 us: on_device(): pl.pallas_call(window_kernel, out_shape=to_frame, in_specs=[in_vmem] * 4...]
    pallas_call x1, Pallas kernels: 5.45 us -> 7.05 us  [on_device(): pl.pallas_call(energy_kernel, out_shape=(near_shape, tops_shape, pltpu.HB...]
  transfers between devices with their start and end apart: 1 -> 1, of which waited for: 1 -> 0; matrix products, arithmetic and copies ran while one was open for 0% -> 0% of each run, Pallas kernels for 6% -> 7%
where the time goes in v8:
time: 102 us; the launch traced here: 101 us
  blocking collectives  58.5 us (57%)
  starting transfers between devices  22.9 us (22%)
  Pallas kernels  19.9 us (20%)
    all_to_all x4, blocking collectives, exchange(): lax.all_to_all(copies, axis, split_axis=0, concat_axis=0, tiled=True, axi...  58.5 us
    all_to_all x1, starting transfers between devices, exchange(): lax.all_to_all(copies, axis, split_axis=0, concat_axis=0, tiled=True, axi...  22.9 us
    pallas_call x2, Pallas kernels, on_device(): pl.pallas_call(window_kernel, out_shape=to_frame, in_specs=[in_vmem] * 4...  8.45 us
    pallas_call x1, Pallas kernels, on_device(): pl.pallas_call(energy_kernel, out_shape=(near_shape, tops_shape, pltpu.HB...  7.05 us
  transfers between devices with their start and end apart: 1, of which 0 were waited for; matrix products, arithmetic and copies ran while one was open for 0% of the time, Pallas kernels for 7%

profile of v8, /device:TPU:1, one launch (start us, length us, event | category | flops | bytes accessed | tf_op | source)
XLA Modules:
  0.0 101.4 jit_solution(7201525767186402155)
XLA Ops:
  0.0 1.7 %count_windows.1 = f32[64,4,128]{2,1,0:T(4,128)} custom-call(s32[64]{0:T(128)} %lengths_hbm.3, s32[1,2048]{1,0:T(1,128)} %bitcast.4), custom_call_target="tpu_custom_call" | custom-call | tf_op jit(solution)/shard_map/count_windows/pallas_call | solution.py:296
  1.7 22.9 %all-to-all-start = ((f32[64,4,128]{2,1,0:T(4,128)}), f32[64,4,128]{2,1,0:T(4,128)S(1)}, u32[]{:S(2)}, u32[]{:S(2)}) async-start(f32[64,4,128]{2,1,0:T(4,128)} %count_windows.1), calls=%async_computation | async-start | bytes 262144 | tf_op jit(solution)/shard_map/all_to_all | solution.py:286
  24.5 7.0 %energies.1 = (f32[512,1664]{1,0:T(8,128)S(1)}, f32[16,128]{1,0:T(8,128)S(1)}, f32[512,384]{1,0:T(8,128)}, f32[512,2048]{1,0:T(8,128)}) custom-call(f32[32,512]{1,0:T(8,128)} %bitcast.5, f32[32,512]{1,0:T(8,128)} %bitcast.6, f32[32,2048]{1,0:T(8,128)} %distances_hbm.1), custom_call_target="tpu_custom_call" | custom-call | flops 805306368 | bytes 4194304 | tf_op jit(solution)/shard_map/energies/pallas_call | solution.py:315
  31.6 0.0 all-to-all-done.shared_ref
  31.6 1.4 %first_denominators.1 = (f32[4,128]{1,0:T(4,128)S(1)}, f32[8,16,128]{2,1,0:T(8,128)S(1)}, f32[512,384]{1,0:T(8,128)S(1)}, f32[16,128]{1,0:T(8,128)S(1)}) custom-call(s32[64]{0:T(128)} %lengths_hbm.3, f32[64,4,128]{2,1,0:T(4,128)S(1)} %all-to-all-done.shared_ref, f32[512,1664]{1,0:T(8,128)S(1)} %get-tuple-element.13.near_ref, ...), custom_call_target="tpu_custom_call" | custom-call | tf_op jit(solution)/shard_map/first_denominators/pallas_call | solution.py:350
  33.0 8.7 %all_to_all.25.shared_ref = f32[8,16,128]{2,1,0:T(8,128)S(1)} all-to-all(f32[8,16,128]{2,1,0:T(8,128)S(1)} %get-tuple-element.17), channel_id=1, replica_groups={{256,320,384,448,0,64,128,192},{257,321,385,449,1,65,129,193},{258,322,..., dimensions={0} | all-to-all | bytes 131072 | tf_op jit(solution)/shard_map/all_to_all | solution.py:286
  41.6 4.2 %window_totals.2 = f32[64,4,128]{2,1,0:T(4,128)S(1)} custom-call(f32[8,16,128]{2,1,0:T(8,128)S(1)} %all_to_all.25.shared_ref, f32[512,1664]{1,0:T(8,128)S(1)} %get-tuple-element.13.near_ref, f32[16,128]{1,0:T(8,128)S(1)} %get-tuple-element.18.used_ref, f32[512,384]{1,0:T(8,128)S(1)} %get-tuple-element.19.far_ref, f32[512,2048]{1,0:T(8,128)} %get-tuple-element.16.fall_hbm), custom_call_target="tpu_custom_call" | custom-call | tf_op jit(solution)/shard_map/window_totals/pallas_call | solution.py:360
  45.9 20.3 %all_to_all.26.shared_ref = f32[64,4,128]{2,1,0:T(4,128)S(1)} all-to-all(f32[64,4,128]{2,1,0:T(4,128)S(1)} %window_totals.2), channel_id=1, replica_groups={{34,35,36,37,38,39,40,41,42,43,44,45,46,47,48,49,50,51,52,53,54,55,56,5..., dimensions={0} | all-to-all | bytes 262144 | tf_op jit(solution)/shard_map/all_to_all | solution.py:286
  66.2 0.7 next_denominators.1
  66.9 8.7 %all_to_all.27.shared_ref = f32[8,16,128]{2,1,0:T(8,128)S(1)} all-to-all(f32[8,16,128]{2,1,0:T(8,128)S(1)} %next_denominators.1), channel_id=1, replica_groups={{256,320,384,448,0,64,128,192},{257,321,385,449,1,65,129,193},{258,322,..., dimensions={0} | all-to-all | bytes 131072 | tf_op jit(solution)/shard_map/all_to_all | solution.py:286
  75.6 4.2 %window_totals.3 = f32[64,4,128]{2,1,0:T(4,128)S(1)} custom-call(f32[8,16,128]{2,1,0:T(8,128)S(1)} %all_to_all.27.shared_ref, f32[512,1664]{1,0:T(8,128)S(1)} %get-tuple-element.13.near_ref, f32[16,128]{1,0:T(8,128)S(1)} %get-tuple-element.18.used_ref, f32[512,384]{1,0:T(8,128)S(1)} %get-tuple-element.19.far_ref, f32[512,2048]{1,0:T(8,128)} %get-tuple-element.16.fall_hbm), custom_call_target="tpu_custom_call" | custom-call | tf_op jit(solution)/shard_map/window_totals/pallas_call | solution.py:360
  79.8 20.8 %all_to_all.28.shared_ref = f32[64,4,128]{2,1,0:T(4,128)S(1)} all-to-all(f32[64,4,128]{2,1,0:T(4,128)S(1)} %window_totals.3), channel_id=1, replica_groups={{34,35,36,37,38,39,40,41,42,43,44,45,46,47,48,49,50,51,52,53,54,55,56,5..., dimensions={0} | all-to-all | bytes 262144 | tf_op jit(solution)/shard_map/all_to_all | solution.py:286
  100.7 0.7 free_energies.1
Async XLA Ops:
  1.7 29.9 %all-to-all-start = ((f32[64,4,128]{2,1,0:T(4,128)}), f32[64,4,128]{2,1,0:T(4,128)S(1)}, u32[]{:S(2)}, u32[]{:S(2)}) async-start(f32[64,4,128]{2,1,0:T(4,128)} %count_windows.1), calls=%async_computation | async-start | bytes 262144 | tf_op jit(solution)/shard_map/all_to_all | solution.py:286

commit v9 on v8

--- a/solution.py
+++ b/solution.py
@@ -17,7 +17,7 @@
 floor_value = -1e30
 log2_e = 1.0 / math.log(2.0)
 FAR = 384
-FIRST = {"frame": 34, "win": 4}
+FIRST = {"frame": 34, "win": 5}
 least_sum = 2.0**-85
 most_rate = 2.0**99
 

time: 102 us -> 101 us (level)
  no operation moved by 1% of the time
where the time goes in v9:
time: 101 us
  blocking collectives  57.8 us (57%)
  starting transfers between devices  22.9 us (23%)
  Pallas kernels  19.9 us (20%)
    all_to_all x4, blocking collectives, exchange(): lax.all_to_all(copies, axis, split_axis=0, concat_axis=0, tiled=True, axi...  57.8 us
    all_to_all x1, starting transfers between devices, exchange(): lax.all_to_all(copies, axis, split_axis=0, concat_axis=0, tiled=True, axi...  22.9 us
    pallas_call x2, Pallas kernels, on_device(): pl.pallas_call(window_kernel, out_shape=to_frame, in_specs=[in_vmem] * 4...  8.45 us
    pallas_call x1, Pallas kernels, on_device(): pl.pallas_call(energy_kernel, out_shape=(near_shape, tops_shape, pltpu.HB...  7.05 us
  transfers between devices with their start and end apart: 1, of which 0 were waited for; matrix products, arithmetic and copies ran while one was open for 0% of the time, Pallas kernels for 7%

profile of v9, /device:TPU:1, one launch (start us, length us, event | category | flops | bytes accessed | tf_op | source)
XLA Modules:
  0.0 100.7 jit_solution(13082923206125254694)
XLA Ops:
  0.0 1.7 %count_windows.1 = f32[64,4,128]{2,1,0:T(4,128)} custom-call(s32[64]{0:T(128)} %lengths_hbm.3, s32[1,2048]{1,0:T(1,128)} %bitcast.4), custom_call_target="tpu_custom_call" | custom-call | tf_op jit(solution)/shard_map/count_windows/pallas_call | solution.py:296
  1.7 22.9 %all-to-all-start = ((f32[64,4,128]{2,1,0:T(4,128)}), f32[64,4,128]{2,1,0:T(4,128)S(1)}, u32[]{:S(2)}, u32[]{:S(2)}) async-start(f32[64,4,128]{2,1,0:T(4,128)} %count_windows.1), calls=%async_computation | async-start | bytes 262144 | tf_op jit(solution)/shard_map/all_to_all | solution.py:286
  24.5 7.0 %energies.1 = (f32[512,1664]{1,0:T(8,128)S(1)}, f32[16,128]{1,0:T(8,128)S(1)}, f32[512,384]{1,0:T(8,128)}, f32[512,2048]{1,0:T(8,128)}) custom-call(f32[32,512]{1,0:T(8,128)} %bitcast.5, f32[32,512]{1,0:T(8,128)} %bitcast.6, f32[32,2048]{1,0:T(8,128)} %distances_hbm.1), custom_call_target="tpu_custom_call" | custom-call | flops 805306368 | bytes 4194304 | tf_op jit(solution)/shard_map/energies/pallas_call | solution.py:315
  31.6 0.0 all-to-all-done.shared_ref
  31.6 1.4 %first_denominators.1 = (f32[4,128]{1,0:T(4,128)S(1)}, f32[8,16,128]{2,1,0:T(8,128)S(1)}, f32[512,384]{1,0:T(8,128)S(1)}, f32[16,128]{1,0:T(8,128)S(1)}) custom-call(s32[64]{0:T(128)} %lengths_hbm.3, f32[64,4,128]{2,1,0:T(4,128)S(1)} %all-to-all-done.shared_ref, f32[512,1664]{1,0:T(8,128)S(1)} %get-tuple-element.13.near_ref, ...), custom_call_target="tpu_custom_call" | custom-call | tf_op jit(solution)/shard_map/first_denominators/pallas_call | solution.py:350
  33.0 8.6 %all_to_all.25.shared_ref = f32[8,16,128]{2,1,0:T(8,128)S(1)} all-to-all(f32[8,16,128]{2,1,0:T(8,128)S(1)} %get-tuple-element.17), channel_id=1, replica_groups={{320,384,448,0,64,128,192,256},{321,385,449,1,65,129,193,257},{322,386,..., dimensions={0} | all-to-all | bytes 131072 | tf_op jit(solution)/shard_map/all_to_all | solution.py:286
  41.6 4.2 %window_totals.2 = f32[64,4,128]{2,1,0:T(4,128)S(1)} custom-call(f32[8,16,128]{2,1,0:T(8,128)S(1)} %all_to_all.25.shared_ref, f32[512,1664]{1,0:T(8,128)S(1)} %get-tuple-element.13.near_ref, f32[16,128]{1,0:T(8,128)S(1)} %get-tuple-element.18.used_ref, f32[512,384]{1,0:T(8,128)S(1)} %get-tuple-element.19.far_ref, f32[512,2048]{1,0:T(8,128)} %get-tuple-element.16.fall_hbm), custom_call_target="tpu_custom_call" | custom-call | tf_op jit(solution)/shard_map/window_totals/pallas_call | solution.py:360
  45.8 20.4 %all_to_all.26.shared_ref = f32[64,4,128]{2,1,0:T(4,128)S(1)} all-to-all(f32[64,4,128]{2,1,0:T(4,128)S(1)} %window_totals.2), channel_id=1, replica_groups={{34,35,36,37,38,39,40,41,42,43,44,45,46,47,48,49,50,51,52,53,54,55,56,5..., dimensions={0} | all-to-all | bytes 262144 | tf_op jit(solution)/shard_map/all_to_all | solution.py:286
  66.2 0.7 next_denominators.1
  66.9 8.0 %all_to_all.27.shared_ref = f32[8,16,128]{2,1,0:T(8,128)S(1)} all-to-all(f32[8,16,128]{2,1,0:T(8,128)S(1)} %next_denominators.1), channel_id=1, replica_groups={{320,384,448,0,64,128,192,256},{321,385,449,1,65,129,193,257},{322,386,..., dimensions={0} | all-to-all | bytes 131072 | tf_op jit(solution)/shard_map/all_to_all | solution.py:286
  74.9 4.2 %window_totals.3 = f32[64,4,128]{2,1,0:T(4,128)S(1)} custom-call(f32[8,16,128]{2,1,0:T(8,128)S(1)} %all_to_all.27.shared_ref, f32[512,1664]{1,0:T(8,128)S(1)} %get-tuple-element.13.near_ref, f32[16,128]{1,0:T(8,128)S(1)} %get-tuple-element.18.used_ref, f32[512,384]{1,0:T(8,128)S(1)} %get-tuple-element.19.far_ref, f32[512,2048]{1,0:T(8,128)} %get-tuple-element.16.fall_hbm), custom_call_target="tpu_custom_call" | custom-call | tf_op jit(solution)/shard_map/window_totals/pallas_call | solution.py:360
  79.1 20.9 %all_to_all.28.shared_ref = f32[64,4,128]{2,1,0:T(4,128)S(1)} all-to-all(f32[64,4,128]{2,1,0:T(4,128)S(1)} %window_totals.3), channel_id=1, replica_groups={{34,35,36,37,38,39,40,41,42,43,44,45,46,47,48,49,50,51,52,53,54,55,56,5..., dimensions={0} | all-to-all | bytes 262144 | tf_op jit(solution)/shard_map/all_to_all | solution.py:286
  100.0 0.7 free_energies.1
Async XLA Ops:
  1.7 29.9 %all-to-all-start = ((f32[64,4,128]{2,1,0:T(4,128)}), f32[64,4,128]{2,1,0:T(4,128)S(1)}, u32[]{:S(2)}, u32[]{:S(2)}) async-start(f32[64,4,128]{2,1,0:T(4,128)} %count_windows.1), calls=%async_computation | async-start | bytes 262144 | tf_op jit(solution)/shard_map/all_to_all | solution.py:286
